TPU v7x, 32 devices: a whole 2x2x4 slice. The times are simulated.
32 devices in a mesh: grp: 1, col: 32 (over z, y, x, core).
Axes of the slice: x: 2, y: 2, z: 4, core: 2. Of those that a mesh axis runs over, the one named last changes fastest.
Arguments:
- pair: bfloat16 [16, 1024, 128], P('grp', 'col'), may hold values from -6 to 6
- w_query: bfloat16 [128, 128], replicated, may hold values from -0.5 to 0.5
- w_kv: bfloat16 [128, 256], replicated, may hold values from -0.5 to 0.5
- w_gate: bfloat16 [128, 128], replicated, may hold values from -0.5 to 0.5
- w_out: bfloat16 [128, 128], replicated, may hold values from -0.5 to 0.5
- pair_bias: bfloat16 [4, 1024, 1024], P('grp', 'col'), may hold values from -8 to 300
- lengths: int32 [1], P('grp'), may hold values from 512 to 1024
Outputs:
- update: bfloat16 [16, 1024, 128], P('grp', 'col')
All inputs are finite; a program needn't handle non-finite values.
Results may differ from a plain program's by a relative error of at most 0.0081.
Values may be sent and summed in bfloat16 or wider, within the bound.
No kernel may reach another device: no remote copies, remote signals or barrier semaphores. Data moves between devices by JAX's collectives and lax.ppermute only.
A program may use at most 128 MiB of HBM per device.

v0:
```python
import jax
import jax.numpy as jnp
from jax import lax
from jax.sharding import PartitionSpec as P

HEADS = 4


def normalize(pair_block):
    values_f = pair_block.astype(jnp.float32)
    mean_val = jnp.mean(values_f, axis=-1, keepdims=True)
    centred = values_f - mean_val
    variance = jnp.mean(centred * centred, axis=-1, keepdims=True)
    return (centred * lax.rsqrt(variance + 1e-05)).astype(jnp.bfloat16)


def attend(normed, bias_query, key_limit, w_query, w_kv, w_gate, w_out, gather_keys):
    row_count, col_count, chan_count = normed.shape
    head_width = chan_count // HEADS
    queries = (
        jnp.dot(normed, w_query, preferred_element_type=jnp.float32) * head_width ** (-0.5)
    ).astype(jnp.bfloat16)
    queries = queries.reshape(row_count, col_count, HEADS, head_width)
    gate_act = jax.nn.sigmoid(jnp.dot(normed, w_gate, preferred_element_type=jnp.float32))

    def consume(running, segment, offset):
        run_max, run_sum, run_acc = running
        key_value = jnp.dot(segment, w_kv, preferred_element_type=jnp.float32).astype(jnp.bfloat16)
        tile_len = key_value.shape[1]
        key_tile = key_value[:, :, :chan_count].reshape(row_count, tile_len, HEADS, head_width)
        value_tile = key_value[:, :, chan_count:].reshape(row_count, tile_len, HEADS, head_width)
        scores = jnp.einsum(
            "rjhd,rkhd->rhjk", queries, key_tile, preferred_element_type=jnp.float32
        )
        bias_part = lax.dynamic_slice_in_dim(bias_query, offset, tile_len, 2).astype(jnp.float32)
        key_pos = offset + jnp.arange(tile_len, dtype=jnp.int32)
        key_mask = jnp.where(key_pos < key_limit, 0.0, -1000000000.0).astype(jnp.float32)
        scores = scores + bias_part[None] + key_mask
        new_max = jnp.maximum(run_max, jnp.max(scores, axis=-1))
        rescale = jnp.exp(run_max - new_max)
        expon = jnp.exp(scores - new_max[..., None])
        new_sum = run_sum * rescale + jnp.sum(expon, axis=-1)
        weights = expon.astype(jnp.bfloat16)
        partial_out = jnp.einsum(
            "rhjk,rkhd->rjhd", weights, value_tile, preferred_element_type=jnp.float32
        )
        new_acc = run_acc * jnp.transpose(rescale, (0, 2, 1))[..., None] + partial_out
        return (new_max, new_sum, new_acc)

    def fold_piece(running, segment, offset, project):
        tile_len = segment.shape[1]
        block_len = 512
        block_num = tile_len // block_len
        blocks = jnp.moveaxis(
            segment.reshape(row_count, block_num, block_len, segment.shape[2]), 1, 0
        )

        def advance(state_now, item_pair):
            block_tile, block_idx = item_pair
            return (consume(state_now, block_tile, block_idx * block_len), None)

        final_state, unused = lax.scan(
            advance, running, (blocks, jnp.arange(block_num, dtype=jnp.int32))
        )
        return final_state

    initial = (
        jnp.full((row_count, HEADS, col_count), -1e30, jnp.float32),
        jnp.zeros((row_count, HEADS, col_count), jnp.float32),
        jnp.zeros((row_count, col_count, HEADS, head_width), jnp.float32),
    )
    run_max, run_sum, run_acc = gather_keys(fold_piece, initial)
    attended = run_acc / jnp.transpose(run_sum, (0, 2, 1))[..., None]
    hidden = (gate_act * attended.reshape(row_count, col_count, chan_count)).astype(jnp.bfloat16)
    return jnp.dot(hidden, w_out, preferred_element_type=jnp.float32).astype(jnp.bfloat16)


def on_device(pair, w_query, w_kv, w_gate, w_out, pair_bias, lengths):
    key_limit = lengths[0]
    normed = normalize(pair)
    received = lax.all_to_all(pair_bias, "col", split_axis=2, concat_axis=1, tiled=True)
    bias_query = jnp.transpose(received, (0, 2, 1))

    def gather_keys(fold_piece, initial):
        return fold_piece(
            initial, lax.all_gather(normed, "col", axis=1, tiled=True), jnp.int32(0), True
        )

    return attend(normed, bias_query, key_limit, w_query, w_kv, w_gate, w_out, gather_keys)


def solution(mesh):
    in_specs = (P("grp", "col", None), P(), P(), P(), P(), P("grp", "col", None), P("grp"))
    out_specs = P("grp", "col", None)
    return jax.shard_map(
        on_device, mesh=mesh, in_specs=in_specs, out_specs=out_specs, check_vma=False
    )
```

profile of v0, /device:TPU:0, one launch (start us, length us, event | category | flops | bytes accessed | tf_op | source)
XLA Modules:
  0.0 114.1 jit_solution(4545162258831155141)
XLA Ops:
  6.5 0.0 copy-start
  6.5 0.0 copy-start.5
  6.5 0.0 all-gather.2.cloned.1.call-start
  6.5 1.1 convert_reduce_fusion
  7.6 1.2 %fusion.30 = f32[16,32]{1,0:T(8,128)S(1)} fusion(bf16[16,32,128]{2,1,0:T(8,128)(2,1)} %param.9, f32[16,32]{1,0:T(8,128)S(1)} %broadcast_multiply_fusion), kind=kLoop, calls=%fused_computation.40 | loop fusion | flops 261632 | bytes 135168 | tf_op jit(solution)/shard_map/reduce_sum | solution.py:13
  8.8 1.8 %fusion.31 = bf16[16,32,128]{2,1,0:T(8,128)(2,1)} fusion(bf16[16,32,128]{2,1,0:T(8,128)(2,1)} %param.9, f32[16,32]{1,0:T(8,128)S(1)} %add_rsqrt_fusion, f32[16,32]{1,0:T(8,128)S(1)} %broadcast_multiply_fusion), kind=kLoop, calls=%fused_computation.41 | loop fusion | flops 262144 | bytes 266240 | tf_op jit(solution)/shard_map/convert_element_type | solution.py:14
  10.6 0.0 all-gather.2.cloned.1.call-update
  10.6 1.6 %copy.17 = bf16[4,32,1024]{1,0,2:T(4,128)(2,1)S(1)} copy(bf16[4,32,1024]{2,1,0:T(8,128)(2,1)} %param.14) | data formatting | bytes 524288 | tf_op args[5]
  12.2 1.7 %reshape.48 = bf16[32,2,2048]{2,1,0:T(2,128)(2,1)} reshape(bf16[1024,4,32]{2,1,0:T(4,128)(2,1)S(1)} %bitcast.92) | data formatting | bytes 524288
  13.9 7.3 %all-to-all-start = ((bf16[32,2,2048]{2,1,0:T(2,128)(2,1)}), bf16[32,2,2048]{2,1,0:T(2,128)(2,1)S(1)}, u32[]{:S(2)}, u32[]{:S(2)}) async-start(bf16[32,2,2048]{2,1,0:T(2,128)(2,1)} %reshape.48), calls=%async_computation | async-start | bytes 524288 | tf_op jit(solution)/shard_map/all_to_all | solution.py:81
  21.3 0.0 copy-done
  21.3 1.1 fusion.27
  22.4 0.2 reshape.40
  22.6 0.9 copy.21
  23.5 0.0 copy-done.5
  23.5 0.7 copy.20
  24.3 8.9 %all-to-all-done = bf16[32,2,2048]{2,1,0:T(2,128)(2,1)S(1)} async-done(((bf16[32,2,2048]{2,1,0:T(2,128)(2,1)}), bf16[32,2,2048]{2,1,0:T(2,128)(2,1)S(1)}, u32[]{:S(2)}, u32[]{:S(2)}) %all-to-all-start) | async-done | bytes 262176 | tf_op jit(solution)/shard_map/all_to_all | solution.py:81
  33.2 0.5 reshape.49
  33.7 0.7 copy.18
  34.4 1.1 all_to_all.16
  35.5 42.7 %all-gather.2.cloned.1.call-done = bf16[16,1024,128]{2,1,0:T(8,128)(2,1)} async-done(((bf16[16,32,128]{2,1,0:T(8,128)(2,1)}), bf16[16,1024,128]{2,1,0:T(8,128)(2,1)}) %all-gather.2.cloned.1.call-update) | async-done | bytes 4194320 | tf_op jit(solution)/shard_map/all_gather | solution.py:86
  78.2 26.6 %while.15 = (s32[]{:T(128)}, f32[16,4,32]{2,1,0:T(4,128)S(1)}, f32[16,4,32]{2,1,0:T(4,128)S(1)}, f32[16,32,4,32]{1,3,2,0:T(8,128)S(1)}, bf16[2,16,512,128]{3,2,0...) while((s32[]{:T(128)}, f32[16,4,32]{2,1,0:T(4,128)S(1)}, ...), condition=%wide.region_5.6_spmd.clone, body=%wide.region_2.5_spmd.clone.sunk | while | flops 684996096 | bytes 52896580 | solution.py:62
  78.2 0.0 copy-start.3
  78.2 0.6 dynamic_slice.24
  79.4 0.7 fusion.63
  80.1 0.0 copy-done.3
  80.1 2.9 %convolution_convert_fusion.3 = bf16[16,512,256]{1,2,0:T(8,128)(2,1)S(1)} fusion(bf16[2,16,512,128]{3,2,0,1:T(8,128)(2,1)} %get-tuple-element.254, s32[]{:T(128)} %get-tuple-element.236, bf16[128,256]{0,1:T(8,128)(2,1)} %get-tuple-element.255), kind=kOutput, calls=%fused_computation.6.clone.1 | convolution fusion | flops 538968064 | bytes 6357504 | tf_op jit(solution)/shard_map/while/body/eval_jaxpr/dot_general | solution.py:28
  82.9 0.0 copy-start.2
  83.0 0.3 fusion.64
  83.3 0.7 copy-done.2
  84.0 2.7 %fusion.65 = (f32[16,4,32]{2,1,0:T(4,128)S(1)}, f32[16,4,512,32]{2,3,1,0:T(8,128)}) fusion(f32[512]{0:T(512)S(1)} %fusion.63, f32[4,32,512]{2,1,0:T(8,128)S(1)} %dynamic-slice_convert_fusion.2, bf16[16,32,4,32]{3,1,2,0:T(8,128)(2,1)S(1)} %copy-done.2, bf16[16,512,4,32]{1,3,2,0:T(8,128)(2,1)S(1)} %bitcast.90), kind=kOutput, calls=%fused_computation.5.clone.1 | convolution fusion | flops 70252544 | bytes 6694912 | tf_op jit(solution)/shard_map/while/body/eval_jaxpr/rjhd,rkhd->rhjk/dot_general | solution.py:32
  86.8 0.0 copy-start.1
  86.8 3.4 %fusion.69 = f32[16,32,4,32]{1,3,2,0:T(8,128)S(1)} fusion(bf16[16,512,4,32]{1,3,2,0:T(8,128)(2,1)S(1)} %bitcast.89, f32[16,4,512,32]{2,3,1,0:T(8,128)} %get-tuple-element.219, f32[16,4,32]{2,1,0:T(4,128)S(1)} %get-tuple-element.251, f32[512]{0:T(512)S(1)} %fusion.63, f32[4,32,512]{2,1,0:T(8,128)S(1)} %dynamic-slice_convert_fusion.2, ...), kind=kOutput, calls=%fused_computation.14.clone.1 | convolution fusion | flops 71499776 | bytes 7096321 | tf_op jit(solution)/shard_map/while/body/eval_jaxpr/rhjk,rkhd->rjhd/dot_general | solution.py:44
  90.2 0.0 copy-done.1
  90.2 0.0 copy-start.4
  90.2 1.2 %fusion.67 = f32[16,4,32]{2,1,0:T(4,128)S(1)} fusion(f32[16,4,512,32]{2,3,1,0:T(8,128)S(1)} %copy-done.1, f32[16,4,32]{2,1,0:T(4,128)S(1)} %get-tuple-element.251, f32[512]{0:T(512)S(1)} %fusion.63, f32[4,32,512]{2,1,0:T(8,128)S(1)} %dynamic-slice_convert_fusion.2), kind=kLoop, calls=%fused_computation.4.clone.1 | loop fusion | flops 4192256 | bytes 4474880 | tf_op jit(solution)/shard_map/while/body/eval_jaxpr/reduce_sum | solution.py:42
  91.4 0.1 fusion.68
  91.5 0.0 copy-done.4
  91.5 0.0 copy-start.3
  91.5 0.6 dynamic_slice.24
  92.7 0.7 fusion.63
  93.4 0.0 copy-done.3
  93.4 2.9 %convolution_convert_fusion.3 = bf16[16,512,256]{1,2,0:T(8,128)(2,1)S(1)} fusion(bf16[2,16,512,128]{3,2,0,1:T(8,128)(2,1)} %get-tuple-element.254, s32[]{:T(128)} %get-tuple-element.236, bf16[128,256]{0,1:T(8,128)(2,1)} %get-tuple-element.255), kind=kOutput, calls=%fused_computation.6.clone.1 | convolution fusion | flops 538968064 | bytes 6357504 | tf_op jit(solution)/shard_map/while/body/eval_jaxpr/dot_general | solution.py:28
  96.2 0.0 copy-start.2
  96.2 0.3 fusion.64
  96.6 0.7 copy-done.2
  97.3 2.8 %fusion.65 = (f32[16,4,32]{2,1,0:T(4,128)S(1)}, f32[16,4,512,32]{2,3,1,0:T(8,128)}) fusion(f32[512]{0:T(512)S(1)} %fusion.63, f32[4,32,512]{2,1,0:T(8,128)S(1)} %dynamic-slice_convert_fusion.2, bf16[16,32,4,32]{3,1,2,0:T(8,128)(2,1)S(1)} %copy-done.2, bf16[16,512,4,32]{1,3,2,0:T(8,128)(2,1)S(1)} %bitcast.90), kind=kOutput, calls=%fused_computation.5.clone.1 | convolution fusion | flops 70252544 | bytes 6694912 | tf_op jit(solution)/shard_map/while/body/eval_jaxpr/rjhd,rkhd->rhjk/dot_general | solution.py:32
  100.1 0.0 copy-start.1
  100.1 3.4 %fusion.69 = f32[16,32,4,32]{1,3,2,0:T(8,128)S(1)} fusion(bf16[16,512,4,32]{1,3,2,0:T(8,128)(2,1)S(1)} %bitcast.89, f32[16,4,512,32]{2,3,1,0:T(8,128)} %get-tuple-element.219, f32[16,4,32]{2,1,0:T(4,128)S(1)} %get-tuple-element.251, f32[512]{0:T(512)S(1)} %fusion.63, f32[4,32,512]{2,1,0:T(8,128)S(1)} %dynamic-slice_convert_fusion.2, ...), kind=kOutput, calls=%fused_computation.14.clone.1 | convolution fusion | flops 71499776 | bytes 7096321 | tf_op jit(solution)/shard_map/while/body/eval_jaxpr/rhjk,rkhd->rjhd/dot_general | solution.py:44
  103.5 0.0 copy-done.1
  103.5 0.0 copy-start.4
  103.5 1.2 %fusion.67 = f32[16,4,32]{2,1,0:T(4,128)S(1)} fusion(f32[16,4,512,32]{2,3,1,0:T(8,128)S(1)} %copy-done.1, f32[16,4,32]{2,1,0:T(4,128)S(1)} %get-tuple-element.251, f32[512]{0:T(512)S(1)} %fusion.63, f32[4,32,512]{2,1,0:T(8,128)S(1)} %dynamic-slice_convert_fusion.2), kind=kLoop, calls=%fused_computation.4.clone.1 | loop fusion | flops 4192256 | bytes 4474880 | tf_op jit(solution)/shard_map/while/body/eval_jaxpr/reduce_sum | solution.py:42
  104.7 0.1 fusion.68
  104.8 0.0 copy-done.4
  104.8 0.2 broadcast_divide_fusion
  105.0 0.3 copy.23
  105.3 1.9 %convolution_convert_fusion.1 = bf16[16,32,128]{2,1,0:T(8,128)(2,1)} fusion(f32[16,32,128]{2,1,0:T(8,128)S(1)} %copy.23, bf16[16,32,128]{2,1,0:T(8,128)(2,1)} %fusion.31, bf16[128,128]{1,0:T(8,128)(2,1)} %param.13, bf16[128,128]{1,0:T(8,128)(2,1)} %param.12), kind=kOutput, calls=%fused_computation.34 | convolution fusion | flops 33947648 | bytes 589824 | tf_op jit(solution)/shard_map/dot_general | solution.py:75
  (12 shorter events, 0.1 us)
Async XLA Ops:
  6.5 14.7 %copy-start = (bf16[128,128]{1,0:T(8,128)(2,1)S(1)}, bf16[128,128]{1,0:T(8,128)(2,1)}, u32[]{:S(2)}) copy-start(bf16[128,128]{1,0:T(8,128)(2,1)} %param.10) | copy-start | bytes 98308
  6.5 17.0 %copy-start.5 = (bf16[128,256]{1,0:T(8,128)(2,1)S(1)}, bf16[128,256]{1,0:T(8,128)(2,1)}, u32[]{:S(2)}) copy-start(bf16[128,256]{1,0:T(8,128)(2,1)} %param.11) | copy-start | bytes 196612
  6.5 71.7 %all-gather.2.cloned.1.call-start = ((), (), s32[]{:S(2)}) async-start(), calls=%async_computation.1 | async-start | bytes 4325376 | tf_op jit(solution)/shard_map/all_gather | solution.py:86
  13.9 19.3 %all-to-all-start = ((bf16[32,2,2048]{2,1,0:T(2,128)(2,1)}), bf16[32,2,2048]{2,1,0:T(2,128)(2,1)S(1)}, u32[]{:S(2)}, u32[]{:S(2)}) async-start(bf16[32,2,2048]{2,1,0:T(2,128)(2,1)} %reshape.48), calls=%async_computation | async-start | bytes 524288 | tf_op jit(solution)/shard_map/all_to_all | solution.py:81
  78.2 1.9 %copy-start.3 = (bf16[4,32,1024]{2,1,0:T(8,128)(2,1)}, bf16[4,32,1024]{2,1,0:T(8,128)(2,1)S(1)}, u32[]{:S(2)}) copy-start(bf16[4,32,1024]{2,1,0:T(8,128)(2,1)S(1)} %get-tuple-element.258) | copy-start | bytes 786436 | tf_op jit(solution)/shard_map/while
  82.9 1.0 copy-start.2
  86.8 3.5 %copy-start.1 = (f32[16,4,512,32]{2,3,1,0:T(8,128)S(1)}, f32[16,4,512,32]{2,3,1,0:T(8,128)}, u32[]{:S(2)}) copy-start(f32[16,4,512,32]{2,3,1,0:T(8,128)} %get-tuple-element.219) | copy-start | bytes 12582916 | tf_op jit(solution)/shard_map/while
  90.2 1.3 %copy-start.4 = (bf16[4,32,1024]{2,1,0:T(8,128)(2,1)S(1)}, bf16[4,32,1024]{2,1,0:T(8,128)(2,1)}, u32[]{:S(2)}) copy-start(bf16[4,32,1024]{2,1,0:T(8,128)(2,1)} %copy-done.3) | copy-start | bytes 786436 | tf_op jit(solution)/shard_map/while
  91.5 1.9 %copy-start.3 = (bf16[4,32,1024]{2,1,0:T(8,128)(2,1)}, bf16[4,32,1024]{2,1,0:T(8,128)(2,1)S(1)}, u32[]{:S(2)}) copy-start(bf16[4,32,1024]{2,1,0:T(8,128)(2,1)S(1)} %get-tuple-element.258) | copy-start | bytes 786436 | tf_op jit(solution)/shard_map/while
  96.2 1.0 copy-start.2
  100.1 3.5 %copy-start.1 = (f32[16,4,512,32]{2,3,1,0:T(8,128)S(1)}, f32[16,4,512,32]{2,3,1,0:T(8,128)}, u32[]{:S(2)}) copy-start(f32[16,4,512,32]{2,3,1,0:T(8,128)} %get-tuple-element.219) | copy-start | bytes 12582916 | tf_op jit(solution)/shard_map/while
  103.5 1.3 %copy-start.4 = (bf16[4,32,1024]{2,1,0:T(8,128)(2,1)S(1)}, bf16[4,32,1024]{2,1,0:T(8,128)(2,1)}, u32[]{:S(2)}) copy-start(bf16[4,32,1024]{2,1,0:T(8,128)(2,1)} %copy-done.3) | copy-start | bytes 786436 | tf_op jit(solution)/shard_map/while
Sparse Core Ops, SparseCore 0:
  10.7 67.4 all-gather.1
where the time goes:
time: 115 us; the launch traced here: 114 us
  waiting for transfers between devices  51.7 us (45%)
  matrix products  21.1 us (18%)
  between operations  13.5 us (12%)
  local copies, waits for them, and re-layouts  11.1 us (10%)
  other arithmetic  8.07 us (7%)
  starting transfers between devices  7.33 us (6%)
  loops' own time  1.32 us (1%)
    all_gather x1, waiting for transfers between devices, gather_keys(): lax.all_gather(normed, 'col', axis=1, tiled=True)  42.7 us
    all_to_all x1, waiting for transfers between devices, on_device(): lax.all_to_all(pair_bias, 'col', split_axis=2, concat_axis=1, tiled=True)  8.93 us
    all_to_all x1, starting transfers between devices, on_device(): lax.all_to_all(pair_bias, 'col', split_axis=2, concat_axis=1, tiled=True)  7.33 us
    dot_general x2, matrix products, consume(): jnp.einsum('rhjk,rkhd->rjhd', weights, value_tile, preferred_element_type...  6.85 us
    dot_general x2, matrix products, consume(): jnp.dot(segment, w_kv, preferred_element_type=jnp.float32)  5.72 us
    dot_general x2, matrix products, consume(): jnp.einsum('rjhd,rkhd->rhjk', queries, key_tile, preferred_element_type=j...  5.51 us
    unnamed x9, local copies, waits for them, and re-layouts  5.47 us
    reduce_sum x2, other arithmetic, consume(): new_sum = run_sum * rescale + jnp.sum(expon, axis=-1)  2.38 us
  transfers between devices with their start and end apart: 2, of which 2 were waited for; matrix products, arithmetic and copies ran while one was open for 7% of the time, Pallas kernels for 0%

commit v1 on v0

v1 whole, which is shorter than its diff:
```python
import functools

import jax
import jax.numpy as jnp
from jax import lax
from jax.experimental import pallas as pl
from jax.experimental.pallas import tpu as pltpu
from jax.sharding import PartitionSpec as P

HEADS = 4
F32 = jnp.float32
BF16 = jnp.bfloat16
SMEM = pl.BlockSpec(memory_space=pltpu.SMEM)


def contract_last(a, b):
    return lax.dot_general(a, b, (((1,), (1,)), ((), ())), preferred_element_type=F32)


def normalized(values):
    values_f = values.astype(F32)
    mean_val = jnp.mean(values_f, axis=-1, keepdims=True)
    centred = values_f - mean_val
    variance = jnp.mean(centred * centred, axis=-1, keepdims=True)
    return (centred * lax.rsqrt(variance + 1e-05)).astype(BF16)


def norm_kernel(place, pair_ref, other_ref, block_ref):
    half_rows, width, _ = other_ref.shape
    core = place[1]
    own_at = pl.multiple_of(core * width, width)
    other_at = pl.multiple_of((1 - core) * width, width)
    block_ref[:, pl.ds(own_at, width), :] = normalized(pair_ref[pl.ds(core * half_rows, half_rows)])
    block_ref[:, pl.ds(other_at, width), :] = normalized(other_ref[...])


def query_kernel(block_ref, w_query_ref, w_kv_ref, w_gate_ref, query_ref, gate_ref):
    rows, cols, chans = block_ref.shape
    head_width = chans // HEADS
    tokens = block_ref[...].reshape(rows * cols, chans)
    queries = (
        jnp.dot(tokens, w_query_ref[...], preferred_element_type=F32) * head_width ** (-0.5)
    ).astype(BF16)
    lane_head = lax.broadcasted_iota(jnp.int32, queries.shape, 1) // head_width
    w_key = w_kv_ref[:, :chans]
    for head in range(HEADS):
        masked = jnp.where(lane_head == head, queries, jnp.zeros_like(queries))
        back = contract_last(masked, w_key).astype(BF16)
        query_ref[:, head * cols : (head + 1) * cols, :] = back.reshape(rows, cols, chans)
    gate = jax.nn.sigmoid(jnp.dot(tokens, w_gate_ref[...], preferred_element_type=F32))
    gate_ref[...] = gate.reshape(rows, cols, chans)


def pack_kernel(bias_ref, packed_ref):
    chips, width, lanes = packed_ref.shape
    cols = lanes // HEADS
    for chip in range(chips):
        for head in range(HEADS):
            packed_ref[chip, :, head * cols : (head + 1) * cols] = bias_ref[
                head, :, chip * cols : (chip + 1) * cols
            ]


def bias_kernel(offsets, place, own_ref, other_ref, bias_ref, keys_ref):
    width, lanes = own_ref.shape[1:]
    chip, core, limit = place[0], place[1], place[2]
    steps = (0, 1 + core, 2 - core, 3)
    row_at = lax.broadcasted_iota(jnp.int32, (width, lanes), 0)
    for spot, (far, near) in enumerate(offsets):
        source = chip ^ far ^ steps[near]
        for part_ref, part in ((own_ref, core), (other_ref, 1 - core)):
            first_key = (source * 2 + part) * width
            mask = jnp.where(first_key + row_at < limit, 0.0, -1000000000.0).astype(F32)
            at = pl.multiple_of(spot * 2 * width + part * width, width)
            keys_ref[pl.ds(at, width), :] = part_ref[source].astype(F32) + mask
    bias_ref[...] = keys_ref[...].T


def attend_kernel(place, *refs):
    pieces = refs[:8]
    query_ref, bias_ref, gate_ref, w_kv_ref, w_out_ref, keep_ref, send_ref, out_ref = refs[8:]
    width, chans = keep_ref.shape[1:]
    cols = 2 * width
    head_width = chans // HEADS
    keys = jnp.concatenate([piece[...].reshape(-1, chans) for piece in pieces], axis=0)
    scores = contract_last(query_ref[0], keys) + bias_ref[...]
    top = jnp.max(scores, axis=-1, keepdims=True)
    expon = jnp.exp(scores - top)
    total = jnp.sum(expon, axis=-1, keepdims=True)
    mixed = jnp.dot(expon.astype(BF16), keys, preferred_element_type=F32)
    mixed = (mixed / total).astype(BF16)
    w_value = w_kv_ref[:, chans:]
    lane_head = lax.broadcasted_iota(jnp.int32, (cols, chans), 1) // head_width
    attended = jnp.zeros((cols, chans), F32)
    for head in range(HEADS):
        one = jnp.dot(mixed[head * cols : (head + 1) * cols], w_value, preferred_element_type=F32)
        attended = jnp.where(lane_head == head, one, attended)
    hidden = (gate_ref[0] * attended).astype(BF16)
    out_ref[...] = jnp.dot(hidden, w_out_ref[...], preferred_element_type=F32).astype(BF16)
    core = place[1]
    keep_ref[0] = out_ref[pl.ds(pl.multiple_of(core * width, width), width), :]
    send_ref[0] = out_ref[pl.ds(pl.multiple_of((1 - core) * width, width), width), :]


def join_kernel(place, keep_ref, recv_ref, out_ref):
    half_rows = keep_ref.shape[0]
    core = place[1]
    out_ref[pl.ds(core * half_rows, half_rows)] = keep_ref[...]
    out_ref[pl.ds((1 - core) * half_rows, half_rows)] = recv_ref[...]


def whole(count):
    return [pl.BlockSpec(memory_space=pltpu.VMEM)] * count


def on_device(n_dev, pair, w_query, w_kv, w_gate, w_out, pair_bias, lengths):
    rows, width, chans = pair.shape
    half_rows = rows // 2
    cols = 2 * width
    chips = n_dev // 2
    index = lax.axis_index("col")
    core = index % 2
    place = jnp.stack([index // 2, core, lengths[0]]).astype(jnp.int32)

    def swap(value, chip_xor):
        perm = [(d, ((d // 2) ^ chip_xor(d % 2)) * 2 + d % 2) for d in range(n_dev)]
        return lax.ppermute(value, "col", perm)

    def swap_core(value):
        return lax.ppermute(value, "col", [(d, d ^ 1) for d in range(n_dev)])

    other = swap_core(lax.dynamic_slice_in_dim(pair, (1 - core) * half_rows, half_rows, 0))

    packed = pl.pallas_call(
        pack_kernel,
        out_shape=jax.ShapeDtypeStruct((chips, width, HEADS * cols), BF16),
        name="pack_bias",
    )(pair_bias)

    block = pl.pallas_call(
        norm_kernel,
        in_specs=[SMEM] + whole(2),
        out_shape=jax.ShapeDtypeStruct((half_rows, cols, chans), BF16),
        name="norm",
    )(place, pair, other)

    near = block[None]
    far_offsets = [0]
    bit = 4
    while bit * 2 < chips:
        near = jnp.concatenate([near, swap(near, lambda c: bit)], axis=0)
        far_offsets = far_offsets + [f ^ bit for f in far_offsets]
        bit *= 2
    far = swap(near, lambda c: bit)
    far_twin = [f ^ bit for f in far_offsets]

    def spread(piece):
        first = swap(piece, lambda c: 1 + c)
        second = swap(piece, lambda c: 2 - c)
        third = swap(first, lambda c: 2 - c)
        return [piece, first, second, third]

    pieces = spread(near) + spread(far)
    offsets = [(f, s) for group in (far_offsets, far_twin) for s in range(4) for f in group]

    same_core = [[chip * 2 + c for chip in range(chips)] for c in range(2)]
    own_bias = lax.all_to_all(
        packed, "col", 0, 0, tiled=True, axis_index_groups=same_core
    )
    other_bias = swap_core(own_bias)

    query, gate = pl.pallas_call(
        query_kernel,
        out_shape=(
            jax.ShapeDtypeStruct((half_rows, HEADS * cols, chans), BF16),
            jax.ShapeDtypeStruct((half_rows, cols, chans), F32),
        ),
        name="query",
    )(block, w_query, w_kv, w_gate)

    n_keys = chips * cols
    bias = pl.pallas_call(
        functools.partial(bias_kernel, offsets),
        in_specs=[SMEM] + whole(2),
        out_shape=jax.ShapeDtypeStruct((HEADS * cols, n_keys), F32),
        scratch_shapes=[pltpu.VMEM((n_keys, HEADS * cols), F32)],
        name="bias",
    )(place, own_bias, other_bias)

    piece_spec = pl.BlockSpec((near.shape[0], 1, cols, chans), lambda r: (0, r, 0, 0))

    def row_spec(size):
        return pl.BlockSpec((1, size, chans), lambda r: (r, 0, 0))

    def full_spec(value):
        return pl.BlockSpec(value.shape, lambda r: (0,) * value.ndim)

    keep, send = pl.pallas_call(
        attend_kernel,
        grid=(half_rows,),
        in_specs=[SMEM]
        + [piece_spec] * 8
        + [row_spec(HEADS * cols), full_spec(bias), row_spec(cols), full_spec(w_kv), full_spec(w_out)],
        out_specs=[row_spec(width)] * 2,
        out_shape=[jax.ShapeDtypeStruct((half_rows, width, chans), BF16)] * 2,
        scratch_shapes=[pltpu.VMEM((cols, chans), BF16)],
        name="attend",
    )(place, *pieces, query, bias, gate, w_kv, w_out)

    return pl.pallas_call(
        join_kernel,
        in_specs=[SMEM] + whole(2),
        out_shape=jax.ShapeDtypeStruct(pair.shape, BF16),
        name="join",
    )(place, keep, swap_core(send))


def solution(mesh):
    in_specs = (P("grp", "col", None), P(), P(), P(), P(), P("grp", "col", None), P("grp"))
    out_specs = P("grp", "col", None)
    return jax.shard_map(
        functools.partial(on_device, mesh.shape["col"]),
        mesh=mesh,
        in_specs=in_specs,
        out_specs=out_specs,
        check_vma=False,
    )
```

time: 115 us -> 62.6 us (0.54)
  waiting for transfers between devices: 51.7 us -> 16.5 us
  matrix products: 21.1 us -> 0 us
  Pallas kernels: 0 us -> 19.8 us
  between operations: 13.5 us -> 0.77 us
  starting transfers between devices: 7.33 us -> 19.9 us
  local copies, waits for them, and re-layouts: 11.1 us -> 3.51 us
  other arithmetic: 8.07 us -> 1.49 us
  loops' own time: 1.32 us -> 0 us
    all_gather x1 -> x0, waiting for transfers between devices: 42.7 us -> none  [gather_keys(): lax.all_gather(normed, 'col', axis=1, tiled=True)]
    dot_general x8 -> x0, matrix products: 21.1 us -> none  [the longest x2 6.85 us: consume(): jnp.einsum('rhjk,rkhd->rjhd', weights, value_tile, preferred_element_type...]
    pallas_call x0 -> x6, Pallas kernels: none -> 19.8 us  [the longest x1 9.89 us: on_device(): pl.pallas_call(attend_kernel, grid=(half_rows,), in_specs=[SMEM] + [piece...]
    ppermute x0 -> x11, waiting for transfers between devices: none -> 16.3 us  [the longest x8 14.9 us: swap(): return lax.ppermute(value, 'col', perm)]
    ppermute x0 -> x11, starting transfers between devices: none -> 15 us  [the longest x8 14.5 us: swap(): return lax.ppermute(value, 'col', perm)]
    all_to_all x1, waiting for transfers between devices: 8.93 us -> 0.14 us  [on_device(): lax.all_to_all(packed, 'col', 0, 0, tiled=True, axis_index_groups=same_core)]
    reduce_sum x4 -> x0, other arithmetic: 4.62 us -> none  [the longest x2 2.38 us: consume(): new_sum = run_sum * rescale + jnp.sum(expon, axis=-1)]
    unnamed x9 -> x24, local copies, waits for them, and re-layouts: 5.47 us -> 2.67 us
  transfers between devices with their start and end apart: 2 -> 12, of which waited for: 2 -> 6; matrix products, arithmetic and copies ran while one was open for 7% -> 1% of each run, Pallas kernels for 0% -> 11%
where the time goes in v1:
time: 62.6 us; the launch traced here: 62 us
  starting transfers between devices  19.9 us (32%)
  Pallas kernels  19.8 us (32%)
  waiting for transfers between devices  16.5 us (26%)
  local copies, waits for them, and re-layouts  3.51 us (6%)
  other arithmetic  1.49 us (2%)
  between operations  0.77 us (1%)
    ppermute x8, waiting for transfers between devices, swap(): return lax.ppermute(value, 'col', perm)  14.9 us
    ppermute x8, starting transfers between devices, swap(): return lax.ppermute(value, 'col', perm)  14.5 us
    pallas_call x1, Pallas kernels, on_device(): pl.pallas_call(attend_kernel, grid=(half_rows,), in_specs=[SMEM] + [piece...  9.89 us
    all_to_all x1, starting transfers between devices, on_device(): lax.all_to_all(packed, 'col', 0, 0, tiled=True, axis_index_groups=same_core)  4.84 us
    unnamed x24, local copies, waits for them, and re-layouts  2.67 us
    pallas_call x1, Pallas kernels, on_device(): pl.pallas_call(functools.partial(bias_kernel, offsets), in_specs=[SMEM] +...  2.52 us
    pallas_call x1, Pallas kernels, on_device(): pl.pallas_call(query_kernel, out_shape=(jax.ShapeDtypeStruct((half_rows,...  2.23 us
    pallas_call x1, Pallas kernels, on_device(): pl.pallas_call(pack_kernel, out_shape=jax.ShapeDtypeStruct((chips, width,...  1.86 us
  transfers between devices with their start and end apart: 12, of which 6 were waited for; matrix products, arithmetic and copies ran while one was open for 1% of the time, Pallas kernels for 11%

profile of v1, /device:TPU:0, one launch (start us, length us, event | category | flops | bytes accessed | tf_op | source)
XLA Modules:
  0.0 62.0 jit_solution(15902986716792485583)
XLA Ops:
  0.0 0.8 %constant_dynamic-slice_fusion = bf16[8,32,128]{2,1,0:T(8,128)(2,1)S(1)} fusion(bf16[16,32,128]{2,1,0:T(8,128)(2,1)} %pair_ref.1, s32[]{:T(128)S(6)} %select_n.16), kind=kLoop, calls=%fused_computation.2 | loop fusion | bytes 131076 | tf_op jit(solution)/shard_map/dynamic_slice | solution.py:132
  0.8 0.5 collective-permute-start
  2.0 0.6 pad_add_fusion.place
  2.6 0.0 collective-permute-done.other_ref
  2.6 0.0 copy-start.10
  2.6 0.6 %copy-done.10 = bf16[8,32,128]{2,1,0:T(8,128)(2,1)} copy-done((bf16[8,32,128]{2,1,0:T(8,128)(2,1)}, bf16[8,32,128]{2,1,0:T(8,128)(2,1)S(1)}, u32[]{:S(2)}) %copy-start.10) | copy-done | bytes 65560
  3.2 1.8 %norm.1.block_ref = bf16[8,64,128]{2,1,0:T(8,128)(2,1)} custom-call(s32[3]{0:T(128)} %pad_add_fusion.place, bf16[16,32,128]{2,1,0:T(8,128)(2,1)} %pair_ref.1, bf16[8,32,128]{2,1,0:T(8,128)(2,1)} %copy-done.10), custom_call_target="tpu_custom_call" | custom-call | tf_op jit(solution)/shard_map/norm/pallas_call | solution.py:140
  5.0 2.6 %collective-permute-start.1 = (bf16[1,8,64,128]{3,2,1,0:T(8,128)(2,1)}, bf16[1,8,64,128]{3,2,1,0:T(8,128)(2,1)S(1)}, u32[]{:S(2)}, u32[]{:S(2)}) collective-permute-start(bf16[1,8,64,128]{3,2,1,0:T(8,128)(2,1)} %bitcast.3), channel_id=1, source_target_pairs={{0,8},{1,9},{2,10},{3,11},{4,12},{5,13},{6,14},{7,15},{8,0},{9,1},... | collective-permute-start | bytes 393224 | tf_op jit(solution)/shard_map/ppermute | solution.py:127
  7.6 4.3 %collective-permute-done.1 = bf16[1,8,64,128]{3,2,1,0:T(8,128)(2,1)S(1)} collective-permute-done((bf16[1,8,64,128]{3,2,1,0:T(8,128)(2,1)}, bf16[1,8,64,128]{3,2,1,0:T(8,128)(2,1)S(1)}, u32[]{:S(2)}, u32[]{:S(2)}) %collective-permute-start.1) | collective-permute-done | bytes 131104 | tf_op jit(solution)/shard_map/ppermute | solution.py:127
  11.9 0.9 %pad_maximum_fusion.refs_0_ = bf16[2,8,64,128]{3,2,1,0:T(8,128)(2,1)S(1)} fusion(bf16[1,8,64,128]{3,2,1,0:T(8,128)(2,1)S(1)} %collective-permute-done.1, bf16[1,8,64,128]{3,2,1,0:T(8,128)(2,1)} %bitcast.4), kind=kLoop, calls=%fused_computation | loop fusion | flops 131072 | bytes 524288 | tf_op jit(solution)/shard_map/concatenate | solution.py:151
  12.9 0.0 copy-start
  12.9 2.8 %collective-permute-start.5 = (bf16[2,8,64,128]{3,2,1,0:T(8,128)(2,1)S(1)}, bf16[2,8,64,128]{3,2,1,0:T(8,128)(2,1)S(1)}, u32[]{:S(2)}, u32[]{:S(2)}) collective-permute-start(bf16[2,8,64,128]{3,2,1,0:T(8,128)(2,1)S(1)} %pad_maximum_fusion.refs_0_), channel_id=1, source_target_pairs={{0,16},{1,17},{2,18},{3,19},{4,20},{5,21},{6,22},{7,23},{8,24},{9,... | collective-permute-start | bytes 786440 | tf_op jit(solution)/shard_map/ppermute | solution.py:127
  15.7 1.9 %pack_bias.1 = bf16[16,32,256]{2,1,0:T(8,128)(2,1)} custom-call(bf16[4,32,1024]{2,1,0:T(8,128)(2,1)} %bias_ref.1), custom_call_target="tpu_custom_call" | custom-call | tf_op jit(solution)/shard_map/pack_bias/pallas_call | solution.py:134
  17.6 4.8 %all-to-all-start = ((bf16[16,32,256]{2,1,0:T(8,128)(2,1)}), bf16[16,32,256]{2,1,0:T(8,128)(2,1)S(1)}, u32[]{:S(2)}, u32[]{:S(2)}) async-start(bf16[16,32,256]{2,1,0:T(8,128)(2,1)} %pack_bias.1), calls=%async_computation | async-start | bytes 524288 | tf_op jit(solution)/shard_map/all_to_all | solution.py:167
  22.4 1.9 %collective-permute-start.2 = (bf16[2,8,64,128]{3,2,1,0:T(8,128)(2,1)S(1)}, bf16[2,8,64,128]{3,2,1,0:T(8,128)(2,1)S(1)}, u32[]{:S(2)}, u32[]{:S(2)}) collective-permute-start(bf16[2,8,64,128]{3,2,1,0:T(8,128)(2,1)S(1)} %pad_maximum_fusion.refs_0_), channel_id=1, source_target_pairs={{0,2},{1,5},{2,0},{3,7},{4,6},{5,1},{6,4},{7,3},{8,10},{9,13},{10,... | collective-permute-start | bytes 786440 | tf_op jit(solution)/shard_map/ppermute | solution.py:127
  24.3 7.1 %collective-permute-done.5.refs_4_ = bf16[2,8,64,128]{3,2,1,0:T(8,128)(2,1)S(1)} collective-permute-done((bf16[2,8,64,128]{3,2,1,0:T(8,128)(2,1)S(1)}, bf16[2,8,64,128]{3,2,1,0:T(8,128)(2,1)S(1)}, u32[]{:S(2)}, u32[]{:S(2)}) %collective-permute-start.5) | collective-permute-done | bytes 262176 | tf_op jit(solution)/shard_map/ppermute | solution.py:127
  31.4 0.0 copy-start.2
  31.4 1.5 %collective-permute-start.6 = (bf16[2,8,64,128]{3,2,1,0:T(8,128)(2,1)S(1)}, bf16[2,8,64,128]{3,2,1,0:T(8,128)(2,1)S(1)}, u32[]{:S(2)}, u32[]{:S(2)}) collective-permute-start(bf16[2,8,64,128]{3,2,1,0:T(8,128)(2,1)S(1)} %collective-permute-done.5.refs_4_), channel_id=1, source_target_pairs={{0,2},{1,5},{2,0},{3,7},{4,6},{5,1},{6,4},{7,3},{8,10},{9,13},{10,... | collective-permute-start | bytes 786440 | tf_op jit(solution)/shard_map/ppermute | solution.py:127
  32.9 0.0 copy-done
  32.9 1.5 %collective-permute-start.3 = (bf16[2,8,64,128]{3,2,1,0:T(8,128)(2,1)S(1)}, bf16[2,8,64,128]{3,2,1,0:T(8,128)(2,1)S(1)}, u32[]{:S(2)}, u32[]{:S(2)}) collective-permute-start(bf16[2,8,64,128]{3,2,1,0:T(8,128)(2,1)S(1)} %pad_maximum_fusion.refs_0_), channel_id=1, source_target_pairs={{0,4},{1,3},{2,6},{3,1},{4,0},{5,7},{6,2},{7,5},{8,12},{9,11},{10,... | collective-permute-start | bytes 786440 | tf_op jit(solution)/shard_map/ppermute | solution.py:127
  34.4 0.1 all-to-all-done.own_ref
  34.6 0.0 copy-start.1
  34.6 0.0 collective-permute-start.9
  34.6 0.8 %collective-permute-start.7 = (bf16[2,8,64,128]{3,2,1,0:T(8,128)(2,1)S(1)}, bf16[2,8,64,128]{3,2,1,0:T(8,128)(2,1)S(1)}, u32[]{:S(2)}, u32[]{:S(2)}) collective-permute-start(bf16[2,8,64,128]{3,2,1,0:T(8,128)(2,1)S(1)} %collective-permute-done.5.refs_4_), channel_id=1, source_target_pairs={{0,4},{1,3},{2,6},{3,1},{4,0},{5,7},{6,2},{7,5},{8,12},{9,11},{10,... | collective-permute-start | bytes 786440 | tf_op jit(solution)/shard_map/ppermute | solution.py:127
  35.4 0.0 collective-permute-done.2.refs_1_
  35.4 0.0 copy-start.3
  35.4 1.2 %collective-permute-start.4 = (bf16[2,8,64,128]{3,2,1,0:T(8,128)(2,1)S(1)}, bf16[2,8,64,128]{3,2,1,0:T(8,128)(2,1)S(1)}, u32[]{:S(2)}, u32[]{:S(2)}) collective-permute-start(bf16[2,8,64,128]{3,2,1,0:T(8,128)(2,1)S(1)} %collective-permute-done.2.refs_1_), channel_id=1, source_target_pairs={{0,4},{1,3},{2,6},{3,1},{4,0},{5,7},{6,2},{7,5},{8,12},{9,11},{10,... | collective-permute-start | bytes 786440 | tf_op jit(solution)/shard_map/ppermute | solution.py:127
  36.6 1.4 %collective-permute-done.6.refs_5_ = bf16[2,8,64,128]{3,2,1,0:T(8,128)(2,1)S(1)} collective-permute-done((bf16[2,8,64,128]{3,2,1,0:T(8,128)(2,1)S(1)}, bf16[2,8,64,128]{3,2,1,0:T(8,128)(2,1)S(1)}, u32[]{:S(2)}, u32[]{:S(2)}) %collective-permute-start.6) | collective-permute-done | bytes 262176 | tf_op jit(solution)/shard_map/ppermute | solution.py:127
  38.0 0.0 copy-start.4
  38.0 2.1 %collective-permute-start.8 = (bf16[2,8,64,128]{3,2,1,0:T(8,128)(2,1)S(1)}, bf16[2,8,64,128]{3,2,1,0:T(8,128)(2,1)S(1)}, u32[]{:S(2)}, u32[]{:S(2)}) collective-permute-start(bf16[2,8,64,128]{3,2,1,0:T(8,128)(2,1)S(1)} %collective-permute-done.6.refs_5_), channel_id=1, source_target_pairs={{0,4},{1,3},{2,6},{3,1},{4,0},{5,7},{6,2},{7,5},{8,12},{9,11},{10,... | collective-permute-start | bytes 786440 | tf_op jit(solution)/shard_map/ppermute | solution.py:127
  40.2 2.2 %query.1 = (bf16[8,256,128]{2,1,0:T(8,128)(2,1)}, f32[8,64,128]{2,1,0:T(8,128)}) custom-call(bf16[8,64,128]{2,1,0:T(8,128)(2,1)} %norm.1.block_ref, bf16[128,128]{1,0:T(8,128)(2,1)} %w_query_ref.1, bf16[128,256]{1,0:T(8,128)(2,1)} %refs_11_.1, bf16[128,128]{1,0:T(8,128)(2,1)} %w_gate_ref.1), custom_call_target="tpu_custom_call" | custom-call | tf_op jit(solution)/shard_map/query/pallas_call | solution.py:172
  42.4 0.0 collective-permute-done.9.other_ref
  42.4 0.0 copy-done.1
  42.4 0.0 copy-start.9
  42.4 0.7 %copy-done.9 = bf16[16,32,256]{2,1,0:T(8,128)(2,1)} copy-done((bf16[16,32,256]{2,1,0:T(8,128)(2,1)}, bf16[16,32,256]{2,1,0:T(8,128)(2,1)S(1)}, u32[]{:S(2)}) %copy-start.9) | copy-done | bytes 262168
  43.1 2.5 %bias.1.refs_9_ = f32[256,1024]{1,0:T(8,128)} custom-call(s32[3]{0:T(128)} %pad_add_fusion.place, bf16[16,32,256]{2,1,0:T(8,128)(2,1)} %copy-done.1, bf16[16,32,256]{2,1,0:T(8,128)(2,1)} %copy-done.9), custom_call_target="tpu_custom_call" | custom-call | tf_op jit(solution)/shard_map/bias/pallas_call | solution.py:182
  45.6 0.0 copy-done.2
  45.6 0.0 copy-done.3
  45.6 0.0 copy-done.4
  45.6 0.0 collective-permute-done.3.refs_2_
  45.6 0.0 copy-start.5
  45.7 0.0 collective-permute-done.7.refs_6_
  45.7 0.0 copy-start.6
  45.7 0.0 collective-permute-done.4.refs_3_
  45.7 0.0 copy-start.7
  45.7 2.0 %collective-permute-done.8.refs_7_ = bf16[2,8,64,128]{3,2,1,0:T(8,128)(2,1)S(1)} collective-permute-done((bf16[2,8,64,128]{3,2,1,0:T(8,128)(2,1)S(1)}, bf16[2,8,64,128]{3,2,1,0:T(8,128)(2,1)S(1)}, u32[]{:S(2)}, u32[]{:S(2)}) %collective-permute-start.8) | collective-permute-done | bytes 262176 | tf_op jit(solution)/shard_map/ppermute | solution.py:127
  47.7 0.0 copy-start.8
  47.7 0.0 copy-done.5
  47.7 0.0 copy-done.6
  47.7 0.0 copy-done.7
  47.7 0.7 %copy-done.8 = bf16[2,8,64,128]{3,2,1,0:T(8,128)(2,1)} copy-done((bf16[2,8,64,128]{3,2,1,0:T(8,128)(2,1)}, bf16[2,8,64,128]{3,2,1,0:T(8,128)(2,1)S(1)}, u32[]{:S(2)}) %copy-start.8) | copy-done | bytes 262168
  48.4 9.9 %attend.1 = (bf16[8,32,128]{2,1,0:T(8,128)(2,1)}, bf16[8,32,128]{2,1,0:T(8,128)(2,1)}) custom-call(s32[3]{0:T(128)} %pad_add_fusion.place, bf16[2,8,64,128]{3,2,1,0:T(8,128)(2,1)} %copy-done, bf16[2,8,64,128]{3,2,1,0:T(8,128)(2,1)} %copy-done.3, bf16[2,8,64,128]{3,2,1,0:T(8,128)(2,1)} %copy-done.5, bf16[2,8,64,128]{3,2,1,0:T(8,128)(2,1)} %copy-done.7, ...), custom_call_target="tpu_custom_call" | custom-call | tf_op jit(solution)/shard_map/attend/pallas_call | solution.py:198
  58.3 0.1 collective-permute-start.10
  58.4 1.5 %collective-permute-done.10.recv_ref = bf16[8,32,128]{2,1,0:T(8,128)(2,1)S(1)} collective-permute-done((bf16[8,32,128]{2,1,0:T(8,128)(2,1)}, bf16[8,32,128]{2,1,0:T(8,128)(2,1)S(1)}, u32[]{:S(2)}, u32[]{:S(2)}) %collective-permute-start.10) | collective-permute-done | bytes 65568 | tf_op jit(solution)/shard_map/ppermute | solution.py:130
  59.8 0.0 copy-start.11
  59.8 0.6 %copy-done.11 = bf16[8,32,128]{2,1,0:T(8,128)(2,1)} copy-done((bf16[8,32,128]{2,1,0:T(8,128)(2,1)}, bf16[8,32,128]{2,1,0:T(8,128)(2,1)S(1)}, u32[]{:S(2)}) %copy-start.11) | copy-done | bytes 65560
  60.4 1.5 %join.1 = bf16[16,32,128]{2,1,0:T(8,128)(2,1)} custom-call(s32[3]{0:T(128)} %pad_add_fusion.place, bf16[8,32,128]{2,1,0:T(8,128)(2,1)} %get-tuple-element.11.keep_ref, bf16[8,32,128]{2,1,0:T(8,128)(2,1)} %copy-done.11), custom_call_target="tpu_custom_call" | custom-call | tf_op jit(solution)/shard_map/join/pallas_call | solution.py:210
Async XLA Ops:
  0.8 1.7 %collective-permute-start = (bf16[8,32,128]{2,1,0:T(8,128)(2,1)S(1)}, bf16[8,32,128]{2,1,0:T(8,128)(2,1)S(1)}, u32[]{:S(2)}, u32[]{:S(2)}) collective-permute-start(bf16[8,32,128]{2,1,0:T(8,128)(2,1)S(1)} %constant_dynamic-slice_fusion), channel_id=1, source_target_pairs={{0,1},{1,0},{2,3},{3,2},{4,5},{5,4},{6,7},{7,6},{8,9},{9,8},{10,11... | collective-permute-start | bytes 196616 | tf_op jit(solution)/shard_map/ppermute | solution.py:130
  2.6 0.6 %copy-start.10 = (bf16[8,32,128]{2,1,0:T(8,128)(2,1)}, bf16[8,32,128]{2,1,0:T(8,128)(2,1)S(1)}, u32[]{:S(2)}) copy-start(bf16[8,32,128]{2,1,0:T(8,128)(2,1)S(1)} %collective-permute-done.other_ref) | copy-start | bytes 196612
  5.0 6.9 %collective-permute-start.1 = (bf16[1,8,64,128]{3,2,1,0:T(8,128)(2,1)}, bf16[1,8,64,128]{3,2,1,0:T(8,128)(2,1)S(1)}, u32[]{:S(2)}, u32[]{:S(2)}) collective-permute-start(bf16[1,8,64,128]{3,2,1,0:T(8,128)(2,1)} %bitcast.3), channel_id=1, source_target_pairs={{0,8},{1,9},{2,10},{3,11},{4,12},{5,13},{6,14},{7,15},{8,0},{9,1},... | collective-permute-start | bytes 393224 | tf_op jit(solution)/shard_map/ppermute | solution.py:127
  12.9 20.0 %copy-start = (bf16[2,8,64,128]{3,2,1,0:T(8,128)(2,1)}, bf16[2,8,64,128]{3,2,1,0:T(8,128)(2,1)S(1)}, u32[]{:S(2)}) copy-start(bf16[2,8,64,128]{3,2,1,0:T(8,128)(2,1)S(1)} %pad_maximum_fusion.refs_0_) | copy-start | bytes 786436
  12.9 18.5 %collective-permute-start.5 = (bf16[2,8,64,128]{3,2,1,0:T(8,128)(2,1)S(1)}, bf16[2,8,64,128]{3,2,1,0:T(8,128)(2,1)S(1)}, u32[]{:S(2)}, u32[]{:S(2)}) collective-permute-start(bf16[2,8,64,128]{3,2,1,0:T(8,128)(2,1)S(1)} %pad_maximum_fusion.refs_0_), channel_id=1, source_target_pairs={{0,16},{1,17},{2,18},{3,19},{4,20},{5,21},{6,22},{7,23},{8,24},{9,... | collective-permute-start | bytes 786440 | tf_op jit(solution)/shard_map/ppermute | solution.py:127
  17.6 17.0 %all-to-all-start = ((bf16[16,32,256]{2,1,0:T(8,128)(2,1)}), bf16[16,32,256]{2,1,0:T(8,128)(2,1)S(1)}, u32[]{:S(2)}, u32[]{:S(2)}) async-start(bf16[16,32,256]{2,1,0:T(8,128)(2,1)} %pack_bias.1), calls=%async_computation | async-start | bytes 524288 | tf_op jit(solution)/shard_map/all_to_all | solution.py:167
  22.4 13.0 %collective-permute-start.2 = (bf16[2,8,64,128]{3,2,1,0:T(8,128)(2,1)S(1)}, bf16[2,8,64,128]{3,2,1,0:T(8,128)(2,1)S(1)}, u32[]{:S(2)}, u32[]{:S(2)}) collective-permute-start(bf16[2,8,64,128]{3,2,1,0:T(8,128)(2,1)S(1)} %pad_maximum_fusion.refs_0_), channel_id=1, source_target_pairs={{0,2},{1,5},{2,0},{3,7},{4,6},{5,1},{6,4},{7,3},{8,10},{9,13},{10,... | collective-permute-start | bytes 786440 | tf_op jit(solution)/shard_map/ppermute | solution.py:127
  31.4 14.2 %copy-start.2 = (bf16[2,8,64,128]{3,2,1,0:T(8,128)(2,1)}, bf16[2,8,64,128]{3,2,1,0:T(8,128)(2,1)S(1)}, u32[]{:S(2)}) copy-start(bf16[2,8,64,128]{3,2,1,0:T(8,128)(2,1)S(1)} %collective-permute-done.5.refs_4_) | copy-start | bytes 786436
  31.4 6.6 %collective-permute-start.6 = (bf16[2,8,64,128]{3,2,1,0:T(8,128)(2,1)S(1)}, bf16[2,8,64,128]{3,2,1,0:T(8,128)(2,1)S(1)}, u32[]{:S(2)}, u32[]{:S(2)}) collective-permute-start(bf16[2,8,64,128]{3,2,1,0:T(8,128)(2,1)S(1)} %collective-permute-done.5.refs_4_), channel_id=1, source_target_pairs={{0,2},{1,5},{2,0},{3,7},{4,6},{5,1},{6,4},{7,3},{8,10},{9,13},{10,... | collective-permute-start | bytes 786440 | tf_op jit(solution)/shard_map/ppermute | solution.py:127
  32.9 12.7 %collective-permute-start.3 = (bf16[2,8,64,128]{3,2,1,0:T(8,128)(2,1)S(1)}, bf16[2,8,64,128]{3,2,1,0:T(8,128)(2,1)S(1)}, u32[]{:S(2)}, u32[]{:S(2)}) collective-permute-start(bf16[2,8,64,128]{3,2,1,0:T(8,128)(2,1)S(1)} %pad_maximum_fusion.refs_0_), channel_id=1, source_target_pairs={{0,4},{1,3},{2,6},{3,1},{4,0},{5,7},{6,2},{7,5},{8,12},{9,11},{10,... | collective-permute-start | bytes 786440 | tf_op jit(solution)/shard_map/ppermute | solution.py:127
  34.6 7.8 %copy-start.1 = (bf16[16,32,256]{2,1,0:T(8,128)(2,1)}, bf16[16,32,256]{2,1,0:T(8,128)(2,1)S(1)}, u32[]{:S(2)}) copy-start(bf16[16,32,256]{2,1,0:T(8,128)(2,1)S(1)} %all-to-all-done.own_ref) | copy-start | bytes 786436
  34.6 7.8 %collective-permute-start.9 = (bf16[16,32,256]{2,1,0:T(8,128)(2,1)S(1)}, bf16[16,32,256]{2,1,0:T(8,128)(2,1)S(1)}, u32[]{:S(2)}, u32[]{:S(2)}) collective-permute-start(bf16[16,32,256]{2,1,0:T(8,128)(2,1)S(1)} %all-to-all-done.own_ref), channel_id=1, source_target_pairs={{0,1},{1,0},{2,3},{3,2},{4,5},{5,4},{6,7},{7,6},{8,9},{9,8},{10,11... | collective-permute-start | bytes 786440 | tf_op jit(solution)/shard_map/ppermute | solution.py:130
  34.6 11.1 %collective-permute-start.7 = (bf16[2,8,64,128]{3,2,1,0:T(8,128)(2,1)S(1)}, bf16[2,8,64,128]{3,2,1,0:T(8,128)(2,1)S(1)}, u32[]{:S(2)}, u32[]{:S(2)}) collective-permute-start(bf16[2,8,64,128]{3,2,1,0:T(8,128)(2,1)S(1)} %collective-permute-done.5.refs_4_), channel_id=1, source_target_pairs={{0,4},{1,3},{2,6},{3,1},{4,0},{5,7},{6,2},{7,5},{8,12},{9,11},{10,... | collective-permute-start | bytes 786440 | tf_op jit(solution)/shard_map/ppermute | solution.py:127
  35.4 10.3 %copy-start.3 = (bf16[2,8,64,128]{3,2,1,0:T(8,128)(2,1)}, bf16[2,8,64,128]{3,2,1,0:T(8,128)(2,1)S(1)}, u32[]{:S(2)}) copy-start(bf16[2,8,64,128]{3,2,1,0:T(8,128)(2,1)S(1)} %collective-permute-done.2.refs_1_) | copy-start | bytes 786436
  35.4 10.3 %collective-permute-start.4 = (bf16[2,8,64,128]{3,2,1,0:T(8,128)(2,1)S(1)}, bf16[2,8,64,128]{3,2,1,0:T(8,128)(2,1)S(1)}, u32[]{:S(2)}, u32[]{:S(2)}) collective-permute-start(bf16[2,8,64,128]{3,2,1,0:T(8,128)(2,1)S(1)} %collective-permute-done.2.refs_1_), channel_id=1, source_target_pairs={{0,4},{1,3},{2,6},{3,1},{4,0},{5,7},{6,2},{7,5},{8,12},{9,11},{10,... | collective-permute-start | bytes 786440 | tf_op jit(solution)/shard_map/ppermute | solution.py:127
  38.0 7.6 %copy-start.4 = (bf16[2,8,64,128]{3,2,1,0:T(8,128)(2,1)}, bf16[2,8,64,128]{3,2,1,0:T(8,128)(2,1)S(1)}, u32[]{:S(2)}) copy-start(bf16[2,8,64,128]{3,2,1,0:T(8,128)(2,1)S(1)} %collective-permute-done.6.refs_5_) | copy-start | bytes 786436
  38.0 9.7 %collective-permute-start.8 = (bf16[2,8,64,128]{3,2,1,0:T(8,128)(2,1)S(1)}, bf16[2,8,64,128]{3,2,1,0:T(8,128)(2,1)S(1)}, u32[]{:S(2)}, u32[]{:S(2)}) collective-permute-start(bf16[2,8,64,128]{3,2,1,0:T(8,128)(2,1)S(1)} %collective-permute-done.6.refs_5_), channel_id=1, source_target_pairs={{0,4},{1,3},{2,6},{3,1},{4,0},{5,7},{6,2},{7,5},{8,12},{9,11},{10,... | collective-permute-start | bytes 786440 | tf_op jit(solution)/shard_map/ppermute | solution.py:127
  42.4 0.7 %copy-start.9 = (bf16[16,32,256]{2,1,0:T(8,128)(2,1)}, bf16[16,32,256]{2,1,0:T(8,128)(2,1)S(1)}, u32[]{:S(2)}) copy-start(bf16[16,32,256]{2,1,0:T(8,128)(2,1)S(1)} %collective-permute-done.9.other_ref) | copy-start | bytes 786436
  45.6 2.1 %copy-start.5 = (bf16[2,8,64,128]{3,2,1,0:T(8,128)(2,1)}, bf16[2,8,64,128]{3,2,1,0:T(8,128)(2,1)S(1)}, u32[]{:S(2)}) copy-start(bf16[2,8,64,128]{3,2,1,0:T(8,128)(2,1)S(1)} %collective-permute-done.3.refs_2_) | copy-start | bytes 786436
  45.7 2.1 %copy-start.6 = (bf16[2,8,64,128]{3,2,1,0:T(8,128)(2,1)}, bf16[2,8,64,128]{3,2,1,0:T(8,128)(2,1)S(1)}, u32[]{:S(2)}) copy-start(bf16[2,8,64,128]{3,2,1,0:T(8,128)(2,1)S(1)} %collective-permute-done.7.refs_6_) | copy-start | bytes 786436
  45.7 2.0 %copy-start.7 = (bf16[2,8,64,128]{3,2,1,0:T(8,128)(2,1)}, bf16[2,8,64,128]{3,2,1,0:T(8,128)(2,1)S(1)}, u32[]{:S(2)}) copy-start(bf16[2,8,64,128]{3,2,1,0:T(8,128)(2,1)S(1)} %collective-permute-done.4.refs_3_) | copy-start | bytes 786436
  47.7 0.7 %copy-start.8 = (bf16[2,8,64,128]{3,2,1,0:T(8,128)(2,1)}, bf16[2,8,64,128]{3,2,1,0:T(8,128)(2,1)S(1)}, u32[]{:S(2)}) copy-start(bf16[2,8,64,128]{3,2,1,0:T(8,128)(2,1)S(1)} %collective-permute-done.8.refs_7_) | copy-start | bytes 786436
  58.3 1.5 %collective-permute-start.10 = (bf16[8,32,128]{2,1,0:T(8,128)(2,1)}, bf16[8,32,128]{2,1,0:T(8,128)(2,1)S(1)}, u32[]{:S(2)}, u32[]{:S(2)}) collective-permute-start(bf16[8,32,128]{2,1,0:T(8,128)(2,1)} %get-tuple-element.12), channel_id=1, source_target_pairs={{0,1},{1,0},{2,3},{3,2},{4,5},{5,4},{6,7},{7,6},{8,9},{9,8},{10,11... | collective-permute-start | bytes 196616 | tf_op jit(solution)/shard_map/ppermute | solution.py:130
  59.8 0.6 %copy-start.11 = (bf16[8,32,128]{2,1,0:T(8,128)(2,1)}, bf16[8,32,128]{2,1,0:T(8,128)(2,1)S(1)}, u32[]{:S(2)}) copy-start(bf16[8,32,128]{2,1,0:T(8,128)(2,1)S(1)} %collective-permute-done.10.recv_ref) | copy-start | bytes 196612

commit v2 on v0

v2 whole, which is shorter than its diff:
```python
import functools
import math

import jax
import jax.numpy as jnp
from jax import lax
from jax.experimental import pallas as pl
from jax.experimental.pallas import tpu as pltpu
from jax.sharding import PartitionSpec as P


HEADS = 4
F32 = jnp.float32
BF16 = jnp.bfloat16
MIB = 1 << 20
LOG2_E = math.log2(math.e)


def vmem_call(kernel, outs, *args, plain=(), in_hbm=False, scratch=(), scalars=(), room=4 * MIB):
    args = [*plain, *(pltpu.with_memory_space_constraint(a, pltpu.VMEM) for a in args)]
    if in_hbm:
        out_shape = [jax.ShapeDtypeStruct(*o) for o in outs]
    else:
        out_shape = [pltpu.VMEM(*o) for o in outs]
    call = pl.pallas_call(
        kernel,
        in_specs=[pl.BlockSpec(memory_space=pltpu.SMEM)] * len(scalars)
        + [pl.BlockSpec(memory_space=pltpu.VMEM)] * len(args),
        out_specs=[pl.BlockSpec(memory_space=pltpu.VMEM)] * len(outs),
        out_shape=out_shape,
        scratch_shapes=scratch,
        compiler_params=pltpu.CompilerParams(vmem_limit_bytes=room),
    )
    results = call(*scalars, *args)
    return results if len(outs) > 1 else results[0]


def my_place():
    index = lax.axis_index("col")
    return index >> 1, index & 1


def contract_last(a, b):
    return lax.dot_general(a, b, (((1,), (1,)), ((), ())), preferred_element_type=F32)


def normalized(values):
    values_f = values.astype(F32)
    mean_val = jnp.mean(values_f, axis=-1, keepdims=True)
    centred = values_f - mean_val
    variance = jnp.mean(centred * centred, axis=-1, keepdims=True)
    return (centred * lax.rsqrt(variance + 1e-05)).astype(BF16)


def early_kernel(stages, pair_ref, bias_ref, own_ref, keep_ref, send_ref, packed_ref):
    half_rows = own_ref.shape[0]
    _, core = my_place()
    own_ref[...] = normalized(pair_ref[pl.ds(core * half_rows, half_rows)])
    pack_bias(stages, bias_ref, keep_ref, send_ref, packed_ref)


def norm_kernel(own_ref, other_ref, block_ref):
    half_rows, width, _ = own_ref.shape
    _, core = my_place()
    own_at = pl.multiple_of(core * width, width)
    other_at = pl.multiple_of((1 - core) * width, width)
    block_ref[0, :, pl.ds(own_at, width), :] = own_ref[...]
    block_ref[0, :, pl.ds(other_at, width), :] = normalized(
        other_ref[pl.ds(core * half_rows, half_rows)]
    )


def stack_kernel(first_ref, second_ref, out_ref):
    count = first_ref.shape[0]
    out_ref[:count] = first_ref[...]
    out_ref[count:] = second_ref[...]


def query_kernel(block_ref, w_query_ref, w_kv_ref, w_gate_ref, query_ref, gate_ref):
    _, rows, cols, chans = block_ref.shape
    head_width = chans // HEADS
    tokens = block_ref[...].reshape(rows * cols, chans)
    queries = (
        jnp.dot(tokens, w_query_ref[...], preferred_element_type=F32) * head_width ** (-0.5)
    ).astype(BF16)
    lane_head = lax.broadcasted_iota(jnp.int32, queries.shape, 1) // head_width
    w_key = w_kv_ref[:, :chans]
    for head in range(HEADS):
        masked = jnp.where(lane_head == head, queries, jnp.zeros_like(queries))
        back = (contract_last(masked, w_key) * LOG2_E).astype(BF16)
        query_ref[:, head * cols : (head + 1) * cols, :] = back.reshape(rows, cols, chans)
    gate = jax.nn.sigmoid(jnp.dot(tokens, w_gate_ref[...], preferred_element_type=F32))
    gate_ref[...] = gate.reshape(rows, cols, chans)


def pack_bias(stages, bias_ref, keep_ref, send_ref, packed_ref):
    half = keep_ref.shape[1]
    chips, _, lanes = packed_ref.shape
    cols = lanes // HEADS
    chip, core = my_place()
    for target in range(chips):
        apart = chip ^ target
        spot = 0
        for stage in stages:
            shift = {"first": core, "second": 1 - core}.get(stage)
            if shift is None:
                shift = stage.bit_length() - 1
            spot = spot * 2 + ((apart >> shift) & 1)
        for head in range(HEADS):
            packed_ref[spot, :, head * cols : (head + 1) * cols] = bias_ref[
                head, :, target * cols : (target + 1) * cols
            ]
    keep_ref[0] = packed_ref[:half]
    send_ref[0] = packed_ref[half:]


def trade_kernel(keep_ref, recv_ref, next_keep_ref, next_send_ref):
    sources, targets = keep_ref.shape[:2]
    half = targets // 2
    next_keep_ref[:sources] = keep_ref[:, :half]
    next_keep_ref[sources:] = recv_ref[:, :half]
    next_send_ref[:sources] = keep_ref[:, half:]
    next_send_ref[sources:] = recv_ref[:, half:]


def bias_kernel(offsets, spots, limit_ref, own_a, own_b, other_a, other_b, bias_ref, keys_ref):
    sources, _, width, lanes = own_a.shape
    chip, core = my_place()
    limit = limit_ref[0]
    steps = (0, 1 + core, 2 - core, 3)
    flipped = (0, 2, 1, 3)
    row_at = lax.broadcasted_iota(jnp.int32, (width, lanes), 0)
    for spot, (far, near) in enumerate(offsets):
        source = chip ^ far ^ steps[near]
        for parts, part, seen in (
            ((own_a, own_b), core, near),
            ((other_a, other_b), 1 - core, flipped[near]),
        ):
            first_key = (source * 2 + part) * width
            mask = jnp.where(first_key + row_at < limit, 0.0, -1000000000.0).astype(F32)
            at = pl.multiple_of(spot * 2 * width + part * width, width)
            held = spots[far, seen]
            value = parts[held // sources][held % sources, 0]
            keys_ref[pl.ds(at, width), :] = (value.astype(F32) + mask) * LOG2_E
    bias_ref[...] = keys_ref[...].T


def attend_rows(key_at, pieces, query_ref, bias_ref, finish):
    rows, lanes, chans = query_ref.shape
    n_keys = sum(piece.shape[0] * piece.shape[2] for piece in pieces)
    step = rows
    while step > 1 and step * lanes * n_keys * 4 > 4 * MIB:
        step //= 2

    def advance(turn, carry):
        at = [turn * step + inner for inner in range(step)]
        keys = [
            jnp.concatenate([piece[:, row].reshape(-1, chans) for piece in pieces], axis=0)
            for row in at
        ]
        bias = bias_ref[:, key_at : key_at + n_keys]
        scores = [contract_last(query_ref[row], key) + bias for row, key in zip(at, keys)]
        tops = [jnp.max(score, axis=-1, keepdims=True) for score in scores]
        expons = [jnp.exp2(score - top) for score, top in zip(scores, tops)]
        totals = [jnp.sum(expon, axis=-1, keepdims=True) for expon in expons]
        mixes = [
            jnp.dot(expon.astype(BF16), key, preferred_element_type=F32)
            for expon, key in zip(expons, keys)
        ]
        for values in zip(at, tops, totals, mixes):
            finish(*values)
        return carry

    if step == rows:
        advance(0, 0)
    else:
        lax.fori_loop(0, rows // step, advance, 0)


def near_kernel(*refs):
    pieces = refs[:4]
    query_ref, bias_ref, top_ref, total_ref, mixed_ref = refs[4:]

    def finish(row, top, total, mixed):
        top_ref[row] = jnp.broadcast_to(top, mixed.shape)
        total_ref[row] = jnp.broadcast_to(total, mixed.shape)
        mixed_ref[row] = mixed

    attend_rows(0, pieces, query_ref, bias_ref, finish)


def far_kernel(*refs):
    pieces = refs[:4]
    (query_ref, bias_ref, top_ref, total_ref, mixed_ref, gate_ref, w_kv_ref, w_out_ref) = refs[4:12]
    keep_ref, send_ref, ready_ref, out_ref = refs[12:]
    rows, cols, chans = gate_ref.shape
    width = keep_ref.shape[1]
    head_width = chans // HEADS
    half_keys = bias_ref.shape[1] // 2

    def finish(row, top, total, mixed):
        old_top = top_ref[row]
        new_top = jnp.maximum(old_top, top)
        old_scale = jnp.exp2(old_top - new_top)
        scale = jnp.exp2(top - new_top)
        inverse = 1.0 / (total_ref[row] * old_scale + total * scale)
        both = mixed_ref[row] * (old_scale * inverse) + mixed * (scale * inverse)
        both = both.astype(BF16)
        for head in range(HEADS):
            ready_ref[head, row] = both[head * cols : (head + 1) * cols]

    attend_rows(half_keys, pieces, query_ref, bias_ref, finish)

    w_value = w_kv_ref[:, chans:]
    lane_head = lax.broadcasted_iota(jnp.int32, w_value.shape, 1) // head_width
    values = [jnp.where(lane_head == h, w_value, jnp.zeros_like(w_value)) for h in range(HEADS)]
    ready = [ready_ref[h].reshape(rows * cols, chans) for h in range(HEADS)]
    attended = jnp.dot(
        jnp.concatenate(ready, axis=1), jnp.concatenate(values, axis=0), preferred_element_type=F32
    )
    hidden = (gate_ref[...].reshape(rows * cols, chans) * attended).astype(BF16)
    update = jnp.dot(hidden, w_out_ref[...], preferred_element_type=F32).astype(BF16)
    out_ref[...] = update.reshape(rows, cols, chans)
    _, core = my_place()
    keep_ref[...] = out_ref[:, pl.ds(pl.multiple_of(core * width, width), width), :]
    send_ref[...] = out_ref[:, pl.ds(pl.multiple_of((1 - core) * width, width), width), :]


def join_kernel(keep_ref, recv_ref, out_ref):
    half_rows = keep_ref.shape[0]
    _, core = my_place()
    out_ref[pl.ds(core * half_rows, half_rows)] = keep_ref[...]
    out_ref[pl.ds((1 - core) * half_rows, half_rows)] = recv_ref[...]


def on_device(n_dev, pair, w_query, w_kv, w_gate, w_out, pair_bias, lengths):
    rows, width, chans = pair.shape
    half_rows = rows // 2
    cols = 2 * width
    lanes = HEADS * cols
    chips = n_dev // 2

    def swap(value, stage):
        def partner(d):
            apart = {"first": 1 + d % 2, "second": 2 - d % 2}.get(stage, stage)
            return ((d // 2) ^ apart) * 2 + d % 2

        return lax.ppermute(value, "col", [(d, partner(d)) for d in range(n_dev)])

    def swap_core(value):
        return lax.ppermute(value, "col", [(d, d ^ 1) for d in range(n_dev)])

    def spread(piece):
        first = swap(piece, "first")
        second = swap(piece, "second")
        third = swap(first, "second")
        return [piece, first, second, third]

    far_bits, stages = travel(n_dev)

    other = swap_core(pair)
    half_targets = ((1, chips // 2, width, lanes), BF16)
    own, keep_bias, send_bias = vmem_call(
        functools.partial(early_kernel, stages),
        [((half_rows, width, chans), BF16), half_targets, half_targets],
        plain=[pair, pair_bias],
        scratch=[pltpu.VMEM((chips, width, lanes), BF16)],
        room=4 * MIB + 4 * chips * width * lanes,
    )
    near = vmem_call(norm_kernel, [((1, half_rows, cols, chans), BF16)], own, other)
    block = near

    near_offsets = [0]
    for bit in far_bits[:0:-1]:
        arrived = swap(near, bit)
        shape = (2 * near.shape[0],) + near.shape[1:]
        near = vmem_call(stack_kernel, [(shape, BF16)], near, arrived)
        near_offsets = near_offsets + [f ^ bit for f in near_offsets]
    far = swap(near, far_bits[0])
    far_offsets = [f ^ far_bits[0] for f in near_offsets]

    near_pieces = spread(near)
    far_pieces = spread(far)
    offsets = [(f, s) for group in (near_offsets, far_offsets) for s in range(4) for f in group]

    for stage in stages[:-1]:
        recv_bias = swap(send_bias, stage)
        sources, targets = keep_bias.shape[:2]
        shape = (2 * sources, targets // 2, width, lanes)
        keep_bias, send_bias = vmem_call(trade_kernel, [(shape, BF16)] * 2, keep_bias, recv_bias)
    recv_bias = swap(send_bias, stages[-1])
    spots = {}
    for held in range(chips):
        taken = [stage for k, stage in enumerate(stages) if held >> k & 1]
        near_step = ("first" in taken) + 2 * ("second" in taken)
        spots[sum(t for t in taken if not isinstance(t, str)), near_step] = held

    query, gate = vmem_call(
        query_kernel,
        [((half_rows, lanes, chans), BF16), ((half_rows, cols, chans), F32)],
        block, w_query, w_kv, w_gate,
    )
    n_keys = chips * cols
    bias = vmem_call(
        functools.partial(bias_kernel, offsets, spots),
        [((lanes, n_keys), F32)],
        keep_bias, recv_bias,
        swap_core(keep_bias), swap_core(recv_bias),
        scratch=[pltpu.VMEM((n_keys, lanes), F32)],
        scalars=[lengths],
        room=4 * MIB + 3 * n_keys * lanes * 4,
    )
    state = vmem_call(
        near_kernel,
        [((half_rows, lanes, chans), F32)] * 3,
        *near_pieces, query, bias,
        room=24 * MIB,
    )
    keep, send = vmem_call(
        far_kernel,
        [((half_rows, width, chans), BF16)] * 2,
        *far_pieces, query, bias, *state, gate, w_kv, w_out,
        room=24 * MIB,
        scratch=[
            pltpu.VMEM((HEADS, half_rows, cols, chans), BF16),
            pltpu.VMEM((half_rows, cols, chans), BF16),
        ],
    )
    return vmem_call(join_kernel, [(pair.shape, BF16)], keep, swap_core(send), in_hbm=True)


def travel(n_dev):
    chips = n_dev // 2
    far_bits = [4 << k for k in range((chips // 4).bit_length() - 1)]
    return far_bits, far_bits[:-1] + ["first", "second"] + far_bits[-1:]


def solution(mesh):
    n_dev = mesh.shape["col"]
    in_specs = (P("grp", "col", None), P(), P(), P(), P(), P("grp", "col", None), P("grp"))
    out_specs = P("grp", "col", None)

    def body(*args):
        return on_device(n_dev, *args)

    return jax.shard_map(
        body, mesh=mesh, in_specs=in_specs, out_specs=out_specs, check_vma=False
    )
```

time: 115 us -> 48.4 us (0.42)
  waiting for transfers between devices: 51.7 us -> 20.5 us
  matrix products: 21.1 us -> 0 us
  between operations: 13.5 us -> 0.78 us
  starting transfers between devices: 7.33 us -> 19.1 us
  local copies, waits for them, and re-layouts: 11.1 us -> 1.87 us
  other arithmetic: 8.07 us -> 0 us
  Pallas kernels: 0 us -> 5.87 us
  loops' own time: 1.32 us -> 0 us
    all_gather x1 -> x0, waiting for transfers between devices: 42.7 us -> none  [gather_keys(): lax.all_gather(normed, 'col', axis=1, tiled=True)]
    dot_general x8 -> x0, matrix products: 21.1 us -> none  [the longest x2 6.85 us: consume(): jnp.einsum('rhjk,rkhd->rjhd', weights, value_tile, preferred_element_type...]
    ppermute x0 -> x16, waiting for transfers between devices: none -> 20.5 us  [the longest x12 19.1 us: swap(): return lax.ppermute(value, 'col', [(d, partner(d)) for d in range(n_dev)])]
    ppermute x0 -> x16, starting transfers between devices: none -> 19.1 us  [the longest x12 18.6 us: swap(): return lax.ppermute(value, 'col', [(d, partner(d)) for d in range(n_dev)])]
    all_to_all x1 -> x0, waiting for transfers between devices: 8.93 us -> none  [on_device(): lax.all_to_all(pair_bias, 'col', split_axis=2, concat_axis=1, tiled=True)]
    all_to_all x1 -> x0, starting transfers between devices: 7.33 us -> none  [on_device(): lax.all_to_all(pair_bias, 'col', split_axis=2, concat_axis=1, tiled=True)]
    pallas_call x0 -> x11, Pallas kernels: none -> 5.87 us  [vmem_call(): results = call(*scalars, *args)]
    reduce_sum x4 -> x0, other arithmetic: 4.62 us -> none  [the longest x2 2.38 us: consume(): new_sum = run_sum * rescale + jnp.sum(expon, axis=-1)]
  transfers between devices with their start and end apart: 2 -> 16, of which waited for: 2 -> 9; matrix products, arithmetic and copies ran while one was open for 7% -> 0% of each run, Pallas kernels for 0% -> 6%
where the time goes in v2:
time: 48.4 us; the launch traced here: 48.2 us
  waiting for transfers between devices  20.5 us (42%)
  starting transfers between devices  19.1 us (39%)
  Pallas kernels  5.87 us (12%)
  local copies, waits for them, and re-layouts  1.87 us (4%)
  between operations  0.78 us (2%)
    ppermute x12, waiting for transfers between devices, swap(): return lax.ppermute(value, 'col', [(d, partner(d)) for d in range(n_dev)])  19.1 us
    ppermute x12, starting transfers between devices, swap(): return lax.ppermute(value, 'col', [(d, partner(d)) for d in range(n_dev)])  18.6 us
    pallas_call x11, Pallas kernels, vmem_call(): results = call(*scalars, *args)  5.87 us
    unnamed x12, local copies, waits for them, and re-layouts  1.87 us
    ppermute x4, waiting for transfers between devices, swap_core(): return lax.ppermute(value, 'col', [(d, d ^ 1) for d in range(n_dev)])  1.42 us
  transfers between devices with their start and end apart: 16, of which 9 were waited for; matrix products, arithmetic and copies ran while one was open for 0% of the time, Pallas kernels for 6%

profile of v2, /device:TPU:0, one launch (start us, length us, event | category | flops | bytes accessed | tf_op | source)
XLA Modules:
  0.0 48.2 jit_solution(3617295326677812229)
XLA Ops:
  0.0 0.5 %collective-permute-start = (bf16[16,32,128]{2,1,0:T(8,128)(2,1)}, bf16[16,32,128]{2,1,0:T(8,128)(2,1)S(1)}, u32[]{:S(2)}, u32[]{:S(2)}) collective-permute-start(bf16[16,32,128]{2,1,0:T(8,128)(2,1)} %pair_ref.1), channel_id=1, source_target_pairs={{0,1},{1,0},{2,3},{3,2},{4,5},{5,4},{6,7},{7,6},{8,9},{9,8},{10,11... | collective-permute-start | bytes 393224 | tf_op jit(solution)/shard_map/ppermute | solution.py:251
  0.5 0.0 copy-start.1
  0.5 0.9 %copy-done.1 = bf16[4,32,1024]{2,1,0:T(8,128)(2,1)S(1)} copy-done((bf16[4,32,1024]{2,1,0:T(8,128)(2,1)S(1)}, bf16[4,32,1024]{2,1,0:T(8,128)(2,1)}, u32[]{:S(2)}) %copy-start.1) | copy-done | bytes 262168
  1.4 0.0 copy-start.2
  1.4 0.9 %copy-done.2 = bf16[16,32,128]{2,1,0:T(8,128)(2,1)S(1)} copy-done((bf16[16,32,128]{2,1,0:T(8,128)(2,1)S(1)}, bf16[16,32,128]{2,1,0:T(8,128)(2,1)}, u32[]{:S(2)}) %copy-start.2) | copy-done | bytes 131096
  2.3 0.3 shard_map.73
  2.7 0.0 collective-permute-done.other_ref
  2.7 0.2 shard_map.74.first_ref.block_ref
  2.9 3.6 %collective-permute-start.1 = (bf16[1,8,64,128]{3,2,1,0:T(8,128)(2,1)S(1)}, bf16[1,8,64,128]{3,2,1,0:T(8,128)(2,1)S(1)}, u32[]{:S(2)}, u32[]{:S(2)}) collective-permute-start(bf16[1,8,64,128]{3,2,1,0:T(8,128)(2,1)S(1)} %shard_map.74.first_ref.block_ref), channel_id=1, source_target_pairs={{0,16},{1,17},{2,18},{3,19},{4,20},{5,21},{6,22},{7,23},{8,24},{9,... | collective-permute-start | bytes 393224 | tf_op jit(solution)/shard_map/ppermute | solution.py:248
  6.6 1.6 %collective-permute-start.6 = (bf16[1,8,32,256]{3,2,1,0:T(8,128)(2,1)S(1)}, bf16[1,8,32,256]{3,2,1,0:T(8,128)(2,1)S(1)}, u32[]{:S(2)}, u32[]{:S(2)}) collective-permute-start(bf16[1,8,32,256]{3,2,1,0:T(8,128)(2,1)S(1)} %get-tuple-element.24), channel_id=1, source_target_pairs={{0,8},{1,9},{2,10},{3,11},{4,12},{5,13},{6,14},{7,15},{8,0},{9,1},... | collective-permute-start | bytes 393224 | tf_op jit(solution)/shard_map/ppermute | solution.py:248
  8.1 5.5 %collective-permute-done.1.second_ref = bf16[1,8,64,128]{3,2,1,0:T(8,128)(2,1)S(1)} collective-permute-done((bf16[1,8,64,128]{3,2,1,0:T(8,128)(2,1)S(1)}, bf16[1,8,64,128]{3,2,1,0:T(8,128)(2,1)S(1)}, u32[]{:S(2)}, u32[]{:S(2)}) %collective-permute-start.1) | collective-permute-done | bytes 131104 | tf_op jit(solution)/shard_map/ppermute | solution.py:248
  13.7 0.7 %collective-permute-start.2 = (bf16[2,8,64,128]{3,2,1,0:T(8,128)(2,1)S(1)}, bf16[2,8,64,128]{3,2,1,0:T(8,128)(2,1)S(1)}, u32[]{:S(2)}, u32[]{:S(2)}) collective-permute-start(bf16[2,8,64,128]{3,2,1,0:T(8,128)(2,1)S(1)} %shard_map.75.refs_0_), channel_id=1, source_target_pairs={{0,8},{1,9},{2,10},{3,11},{4,12},{5,13},{6,14},{7,15},{8,0},{9,1},... | collective-permute-start | bytes 786440 | tf_op jit(solution)/shard_map/ppermute | solution.py:248
  14.4 0.0 collective-permute-done.6.recv_ref
  14.4 1.6 %collective-permute-start.7 = (bf16[2,4,32,256]{3,2,1,0:T(8,128)(2,1)S(1)}, bf16[2,4,32,256]{3,2,1,0:T(8,128)(2,1)S(1)}, u32[]{:S(2)}, u32[]{:S(2)}) collective-permute-start(bf16[2,4,32,256]{3,2,1,0:T(8,128)(2,1)S(1)} %get-tuple-element.26), channel_id=1, source_target_pairs={{0,2},{1,5},{2,0},{3,7},{4,6},{5,1},{6,4},{7,3},{8,10},{9,13},{10,... | collective-permute-start | bytes 393224 | tf_op jit(solution)/shard_map/ppermute | solution.py:248
  15.9 3.5 %collective-permute-done.7.recv_ref = bf16[2,4,32,256]{3,2,1,0:T(8,128)(2,1)S(1)} collective-permute-done((bf16[2,4,32,256]{3,2,1,0:T(8,128)(2,1)S(1)}, bf16[2,4,32,256]{3,2,1,0:T(8,128)(2,1)S(1)}, u32[]{:S(2)}, u32[]{:S(2)}) %collective-permute-start.7) | collective-permute-done | bytes 131104 | tf_op jit(solution)/shard_map/ppermute | solution.py:248
  19.4 1.6 %collective-permute-start.8 = (bf16[4,2,32,256]{3,2,1,0:T(8,128)(2,1)S(1)}, bf16[4,2,32,256]{3,2,1,0:T(8,128)(2,1)S(1)}, u32[]{:S(2)}, u32[]{:S(2)}) collective-permute-start(bf16[4,2,32,256]{3,2,1,0:T(8,128)(2,1)S(1)} %get-tuple-element.28), channel_id=1, source_target_pairs={{0,4},{1,3},{2,6},{3,1},{4,0},{5,7},{6,2},{7,5},{8,12},{9,11},{10,... | collective-permute-start | bytes 393224 | tf_op jit(solution)/shard_map/ppermute | solution.py:248
  21.0 1.5 %collective-permute-start.12 = (bf16[2,8,64,128]{3,2,1,0:T(8,128)(2,1)S(1)}, bf16[2,8,64,128]{3,2,1,0:T(8,128)(2,1)S(1)}, u32[]{:S(2)}, u32[]{:S(2)}) collective-permute-start(bf16[2,8,64,128]{3,2,1,0:T(8,128)(2,1)S(1)} %shard_map.75.refs_0_), channel_id=1, source_target_pairs={{0,2},{1,5},{2,0},{3,7},{4,6},{5,1},{6,4},{7,3},{8,10},{9,13},{10,... | collective-permute-start | bytes 786440 | tf_op jit(solution)/shard_map/ppermute | solution.py:248
  22.5 0.0 collective-permute-done.2.refs_0_
  22.5 0.5 %collective-permute-start.3 = (bf16[2,8,64,128]{3,2,1,0:T(8,128)(2,1)S(1)}, bf16[2,8,64,128]{3,2,1,0:T(8,128)(2,1)S(1)}, u32[]{:S(2)}, u32[]{:S(2)}) collective-permute-start(bf16[2,8,64,128]{3,2,1,0:T(8,128)(2,1)S(1)} %collective-permute-done.2.refs_0_), channel_id=1, source_target_pairs={{0,2},{1,5},{2,0},{3,7},{4,6},{5,1},{6,4},{7,3},{8,10},{9,13},{10,... | collective-permute-start | bytes 786440 | tf_op jit(solution)/shard_map/ppermute | solution.py:248
  23.1 2.8 %collective-permute-done.8.recv_ref = bf16[4,2,32,256]{3,2,1,0:T(8,128)(2,1)S(1)} collective-permute-done((bf16[4,2,32,256]{3,2,1,0:T(8,128)(2,1)S(1)}, bf16[4,2,32,256]{3,2,1,0:T(8,128)(2,1)S(1)}, u32[]{:S(2)}, u32[]{:S(2)}) %collective-permute-start.8) | collective-permute-done | bytes 131104 | tf_op jit(solution)/shard_map/ppermute | solution.py:248
  25.9 0.0 copy-start
  25.9 0.0 copy-start.4
  25.9 0.0 copy-start.5
  25.9 3.4 %collective-permute-start.9 = (bf16[8,1,32,256]{3,2,1,0:T(8,128)(2,1)S(1)}, bf16[8,1,32,256]{3,2,1,0:T(8,128)(2,1)S(1)}, u32[]{:S(2)}, u32[]{:S(2)}) collective-permute-start(bf16[8,1,32,256]{3,2,1,0:T(8,128)(2,1)S(1)} %get-tuple-element.30), channel_id=1, source_target_pairs={{0,16},{1,17},{2,18},{3,19},{4,20},{5,21},{6,22},{7,23},{8,24},{9,... | collective-permute-start | bytes 393224 | tf_op jit(solution)/shard_map/ppermute | solution.py:248
  29.3 0.0 collective-permute-start.10
  29.3 1.5 %collective-permute-start.13 = (bf16[2,8,64,128]{3,2,1,0:T(8,128)(2,1)S(1)}, bf16[2,8,64,128]{3,2,1,0:T(8,128)(2,1)S(1)}, u32[]{:S(2)}, u32[]{:S(2)}) collective-permute-start(bf16[2,8,64,128]{3,2,1,0:T(8,128)(2,1)S(1)} %shard_map.75.refs_0_), channel_id=1, source_target_pairs={{0,4},{1,3},{2,6},{3,1},{4,0},{5,7},{6,2},{7,5},{8,12},{9,11},{10,... | collective-permute-start | bytes 786440 | tf_op jit(solution)/shard_map/ppermute | solution.py:248
  30.9 0.0 collective-permute-done.12.refs_1_
  30.9 0.5 %collective-permute-start.14 = (bf16[2,8,64,128]{3,2,1,0:T(8,128)(2,1)S(1)}, bf16[2,8,64,128]{3,2,1,0:T(8,128)(2,1)S(1)}, u32[]{:S(2)}, u32[]{:S(2)}) collective-permute-start(bf16[2,8,64,128]{3,2,1,0:T(8,128)(2,1)S(1)} %collective-permute-done.12.refs_1_), channel_id=1, source_target_pairs={{0,4},{1,3},{2,6},{3,1},{4,0},{5,7},{6,2},{7,5},{8,12},{9,11},{10,... | collective-permute-start | bytes 786440 | tf_op jit(solution)/shard_map/ppermute | solution.py:248
  31.4 2.3 %collective-permute-done.9.own_b = bf16[8,1,32,256]{3,2,1,0:T(8,128)(2,1)S(1)} collective-permute-done((bf16[8,1,32,256]{3,2,1,0:T(8,128)(2,1)S(1)}, bf16[8,1,32,256]{3,2,1,0:T(8,128)(2,1)S(1)}, u32[]{:S(2)}, u32[]{:S(2)}) %collective-permute-start.9) | collective-permute-done | bytes 131104 | tf_op jit(solution)/shard_map/ppermute | solution.py:248
  33.7 1.5 %collective-permute-start.4 = (bf16[2,8,64,128]{3,2,1,0:T(8,128)(2,1)S(1)}, bf16[2,8,64,128]{3,2,1,0:T(8,128)(2,1)S(1)}, u32[]{:S(2)}, u32[]{:S(2)}) collective-permute-start(bf16[2,8,64,128]{3,2,1,0:T(8,128)(2,1)S(1)} %collective-permute-done.2.refs_0_), channel_id=1, source_target_pairs={{0,4},{1,3},{2,6},{3,1},{4,0},{5,7},{6,2},{7,5},{8,12},{9,11},{10,... | collective-permute-start | bytes 786440 | tf_op jit(solution)/shard_map/ppermute | solution.py:248
  35.2 0.0 collective-permute-done.3.refs_1_
  35.2 0.5 %collective-permute-start.5 = (bf16[2,8,64,128]{3,2,1,0:T(8,128)(2,1)S(1)}, bf16[2,8,64,128]{3,2,1,0:T(8,128)(2,1)S(1)}, u32[]{:S(2)}, u32[]{:S(2)}) collective-permute-start(bf16[2,8,64,128]{3,2,1,0:T(8,128)(2,1)S(1)} %collective-permute-done.3.refs_1_), channel_id=1, source_target_pairs={{0,4},{1,3},{2,6},{3,1},{4,0},{5,7},{6,2},{7,5},{8,12},{9,11},{10,... | collective-permute-start | bytes 786440 | tf_op jit(solution)/shard_map/ppermute | solution.py:248
  35.7 0.0 collective-permute-done.10.other_a
  35.7 0.0 collective-permute-start.11
  36.4 0.0 copy-done
  36.4 0.0 copy-done.4
  36.4 0.0 copy-done.5
  36.4 0.5 shard_map.76
  36.9 0.2 collective-permute-done.11.other_b
  37.1 0.5 shard_map.80.refs_5_
  37.6 0.0 collective-permute-done.13.refs_2_
  37.6 0.9 %collective-permute-done.14.refs_3_ = bf16[2,8,64,128]{3,2,1,0:T(8,128)(2,1)S(1)} collective-permute-done((bf16[2,8,64,128]{3,2,1,0:T(8,128)(2,1)S(1)}, bf16[2,8,64,128]{3,2,1,0:T(8,128)(2,1)S(1)}, u32[]{:S(2)}, u32[]{:S(2)}) %collective-permute-start.14) | collective-permute-done | bytes 262176 | tf_op jit(solution)/shard_map/ppermute | solution.py:248
  38.5 0.0 copy-start.3
  38.5 1.6 %shard_map.81 = (f32[8,256,128]{2,1,0:T(8,128)S(1)}, f32[8,256,128]{2,1,0:T(8,128)S(1)}, f32[8,256,128]{2,1,0:T(8,128)S(1)}) custom-call(bf16[2,8,64,128]{3,2,1,0:T(8,128)(2,1)S(1)} %shard_map.75.refs_0_, bf16[2,8,64,128]{3,2,1,0:T(8,128)(2,1)S(1)} %collective-permute-done.12.refs_1_, bf16[2,8,64,128]{3,2,1,0:T(8,128)(2,1)S(1)} %collective-permute-done.13.refs_2_, ...), custom_call_target="tpu_custom_call" | custom-call | tf_op jit(solution)/shard_map/pallas_call | solution.py:34
  40.1 1.2 %collective-permute-done.4.refs_2_ = bf16[2,8,64,128]{3,2,1,0:T(8,128)(2,1)S(1)} collective-permute-done((bf16[2,8,64,128]{3,2,1,0:T(8,128)(2,1)S(1)}, bf16[2,8,64,128]{3,2,1,0:T(8,128)(2,1)S(1)}, u32[]{:S(2)}, u32[]{:S(2)}) %collective-permute-start.4) | collective-permute-done | bytes 262176 | tf_op jit(solution)/shard_map/ppermute | solution.py:248
  41.3 2.8 %collective-permute-done.5.refs_3_ = bf16[2,8,64,128]{3,2,1,0:T(8,128)(2,1)S(1)} collective-permute-done((bf16[2,8,64,128]{3,2,1,0:T(8,128)(2,1)S(1)}, bf16[2,8,64,128]{3,2,1,0:T(8,128)(2,1)S(1)}, u32[]{:S(2)}, u32[]{:S(2)}) %collective-permute-start.5) | collective-permute-done | bytes 262176 | tf_op jit(solution)/shard_map/ppermute | solution.py:248
  44.1 0.0 copy-done.3
  44.1 2.1 %shard_map.82 = (bf16[8,32,128]{2,1,0:T(8,128)(2,1)S(1)}, bf16[8,32,128]{2,1,0:T(8,128)(2,1)S(1)}) custom-call(bf16[2,8,64,128]{3,2,1,0:T(8,128)(2,1)S(1)} %collective-permute-done.2.refs_0_, bf16[2,8,64,128]{3,2,1,0:T(8,128)(2,1)S(1)} %collective-permute-done.3.refs_1_, bf16[2,8,64,128]{3,2,1,0:T(8,128)(2,1)S(1)} %collective-permute-done.4.refs_2_, ...), custom_call_target="tpu_custom_call" | custom-call | tf_op jit(solution)/shard_map/pallas_call | solution.py:34
  46.2 0.1 collective-permute-start.15
  46.3 1.2 %collective-permute-done.15.recv_ref = bf16[8,32,128]{2,1,0:T(8,128)(2,1)S(1)} collective-permute-done((bf16[8,32,128]{2,1,0:T(8,128)(2,1)S(1)}, bf16[8,32,128]{2,1,0:T(8,128)(2,1)S(1)}, u32[]{:S(2)}, u32[]{:S(2)}) %collective-permute-start.15) | collective-permute-done | bytes 65568 | tf_op jit(solution)/shard_map/ppermute | solution.py:251
  47.5 0.7 %shard_map.83 = bf16[16,32,128]{2,1,0:T(8,128)(2,1)} custom-call(bf16[8,32,128]{2,1,0:T(8,128)(2,1)S(1)} %get-tuple-element.35.keep_ref, bf16[8,32,128]{2,1,0:T(8,128)(2,1)S(1)} %collective-permute-done.15.recv_ref), custom_call_target="tpu_custom_call" | custom-call | tf_op jit(solution)/shard_map/pallas_call | solution.py:34
  (4 shorter events, 0.1 us)
Async XLA Ops:
  0.0 2.7 %collective-permute-start = (bf16[16,32,128]{2,1,0:T(8,128)(2,1)}, bf16[16,32,128]{2,1,0:T(8,128)(2,1)S(1)}, u32[]{:S(2)}, u32[]{:S(2)}) collective-permute-start(bf16[16,32,128]{2,1,0:T(8,128)(2,1)} %pair_ref.1), channel_id=1, source_target_pairs={{0,1},{1,0},{2,3},{3,2},{4,5},{5,4},{6,7},{7,6},{8,9},{9,8},{10,11... | collective-permute-start | bytes 393224 | tf_op jit(solution)/shard_map/ppermute | solution.py:251
  0.5 0.9 %copy-start.1 = (bf16[4,32,1024]{2,1,0:T(8,128)(2,1)S(1)}, bf16[4,32,1024]{2,1,0:T(8,128)(2,1)}, u32[]{:S(2)}) copy-start(bf16[4,32,1024]{2,1,0:T(8,128)(2,1)} %bias_ref.1) | copy-start | bytes 786436
  1.4 0.9 %copy-start.2 = (bf16[16,32,128]{2,1,0:T(8,128)(2,1)S(1)}, bf16[16,32,128]{2,1,0:T(8,128)(2,1)}, u32[]{:S(2)}) copy-start(bf16[16,32,128]{2,1,0:T(8,128)(2,1)} %pair_ref.1) | copy-start | bytes 393220
  2.9 10.7 %collective-permute-start.1 = (bf16[1,8,64,128]{3,2,1,0:T(8,128)(2,1)S(1)}, bf16[1,8,64,128]{3,2,1,0:T(8,128)(2,1)S(1)}, u32[]{:S(2)}, u32[]{:S(2)}) collective-permute-start(bf16[1,8,64,128]{3,2,1,0:T(8,128)(2,1)S(1)} %shard_map.74.first_ref.block_ref), channel_id=1, source_target_pairs={{0,16},{1,17},{2,18},{3,19},{4,20},{5,21},{6,22},{7,23},{8,24},{9,... | collective-permute-start | bytes 393224 | tf_op jit(solution)/shard_map/ppermute | solution.py:248
  6.6 7.8 %collective-permute-start.6 = (bf16[1,8,32,256]{3,2,1,0:T(8,128)(2,1)S(1)}, bf16[1,8,32,256]{3,2,1,0:T(8,128)(2,1)S(1)}, u32[]{:S(2)}, u32[]{:S(2)}) collective-permute-start(bf16[1,8,32,256]{3,2,1,0:T(8,128)(2,1)S(1)} %get-tuple-element.24), channel_id=1, source_target_pairs={{0,8},{1,9},{2,10},{3,11},{4,12},{5,13},{6,14},{7,15},{8,0},{9,1},... | collective-permute-start | bytes 393224 | tf_op jit(solution)/shard_map/ppermute | solution.py:248
  13.7 8.9 %collective-permute-start.2 = (bf16[2,8,64,128]{3,2,1,0:T(8,128)(2,1)S(1)}, bf16[2,8,64,128]{3,2,1,0:T(8,128)(2,1)S(1)}, u32[]{:S(2)}, u32[]{:S(2)}) collective-permute-start(bf16[2,8,64,128]{3,2,1,0:T(8,128)(2,1)S(1)} %shard_map.75.refs_0_), channel_id=1, source_target_pairs={{0,8},{1,9},{2,10},{3,11},{4,12},{5,13},{6,14},{7,15},{8,0},{9,1},... | collective-permute-start | bytes 786440 | tf_op jit(solution)/shard_map/ppermute | solution.py:248
  14.4 5.0 %collective-permute-start.7 = (bf16[2,4,32,256]{3,2,1,0:T(8,128)(2,1)S(1)}, bf16[2,4,32,256]{3,2,1,0:T(8,128)(2,1)S(1)}, u32[]{:S(2)}, u32[]{:S(2)}) collective-permute-start(bf16[2,4,32,256]{3,2,1,0:T(8,128)(2,1)S(1)} %get-tuple-element.26), channel_id=1, source_target_pairs={{0,2},{1,5},{2,0},{3,7},{4,6},{5,1},{6,4},{7,3},{8,10},{9,13},{10,... | collective-permute-start | bytes 393224 | tf_op jit(solution)/shard_map/ppermute | solution.py:248
  19.4 6.4 %collective-permute-start.8 = (bf16[4,2,32,256]{3,2,1,0:T(8,128)(2,1)S(1)}, bf16[4,2,32,256]{3,2,1,0:T(8,128)(2,1)S(1)}, u32[]{:S(2)}, u32[]{:S(2)}) collective-permute-start(bf16[4,2,32,256]{3,2,1,0:T(8,128)(2,1)S(1)} %get-tuple-element.28), channel_id=1, source_target_pairs={{0,4},{1,3},{2,6},{3,1},{4,0},{5,7},{6,2},{7,5},{8,12},{9,11},{10,... | collective-permute-start | bytes 393224 | tf_op jit(solution)/shard_map/ppermute | solution.py:248
  21.0 9.8 %collective-permute-start.12 = (bf16[2,8,64,128]{3,2,1,0:T(8,128)(2,1)S(1)}, bf16[2,8,64,128]{3,2,1,0:T(8,128)(2,1)S(1)}, u32[]{:S(2)}, u32[]{:S(2)}) collective-permute-start(bf16[2,8,64,128]{3,2,1,0:T(8,128)(2,1)S(1)} %shard_map.75.refs_0_), channel_id=1, source_target_pairs={{0,2},{1,5},{2,0},{3,7},{4,6},{5,1},{6,4},{7,3},{8,10},{9,13},{10,... | collective-permute-start | bytes 786440 | tf_op jit(solution)/shard_map/ppermute | solution.py:248
  22.5 12.7 %collective-permute-start.3 = (bf16[2,8,64,128]{3,2,1,0:T(8,128)(2,1)S(1)}, bf16[2,8,64,128]{3,2,1,0:T(8,128)(2,1)S(1)}, u32[]{:S(2)}, u32[]{:S(2)}) collective-permute-start(bf16[2,8,64,128]{3,2,1,0:T(8,128)(2,1)S(1)} %collective-permute-done.2.refs_0_), channel_id=1, source_target_pairs={{0,2},{1,5},{2,0},{3,7},{4,6},{5,1},{6,4},{7,3},{8,10},{9,13},{10,... | collective-permute-start | bytes 786440 | tf_op jit(solution)/shard_map/ppermute | solution.py:248
  25.9 10.5 %copy-start = (bf16[128,256]{1,0:T(8,128)(2,1)S(1)}, bf16[128,256]{1,0:T(8,128)(2,1)}, u32[]{:S(2)}) copy-start(bf16[128,256]{1,0:T(8,128)(2,1)} %refs_10_.1) | copy-start | bytes 196612
  25.9 10.5 %copy-start.4 = (bf16[128,128]{1,0:T(8,128)(2,1)S(1)}, bf16[128,128]{1,0:T(8,128)(2,1)}, u32[]{:S(2)}) copy-start(bf16[128,128]{1,0:T(8,128)(2,1)} %w_query_ref.1) | copy-start | bytes 98308
  25.9 10.5 %copy-start.5 = (bf16[128,128]{1,0:T(8,128)(2,1)S(1)}, bf16[128,128]{1,0:T(8,128)(2,1)}, u32[]{:S(2)}) copy-start(bf16[128,128]{1,0:T(8,128)(2,1)} %w_gate_ref.1) | copy-start | bytes 98308
  25.9 7.8 %collective-permute-start.9 = (bf16[8,1,32,256]{3,2,1,0:T(8,128)(2,1)S(1)}, bf16[8,1,32,256]{3,2,1,0:T(8,128)(2,1)S(1)}, u32[]{:S(2)}, u32[]{:S(2)}) collective-permute-start(bf16[8,1,32,256]{3,2,1,0:T(8,128)(2,1)S(1)} %get-tuple-element.30), channel_id=1, source_target_pairs={{0,16},{1,17},{2,18},{3,19},{4,20},{5,21},{6,22},{7,23},{8,24},{9,... | collective-permute-start | bytes 393224 | tf_op jit(solution)/shard_map/ppermute | solution.py:248
  29.3 6.4 %collective-permute-start.10 = (bf16[8,1,32,256]{3,2,1,0:T(8,128)(2,1)S(1)}, bf16[8,1,32,256]{3,2,1,0:T(8,128)(2,1)S(1)}, u32[]{:S(2)}, u32[]{:S(2)}) collective-permute-start(bf16[8,1,32,256]{3,2,1,0:T(8,128)(2,1)S(1)} %get-tuple-element.29.own_a), channel_id=1, source_target_pairs={{0,1},{1,0},{2,3},{3,2},{4,5},{5,4},{6,7},{7,6},{8,9},{9,8},{10,11... | collective-permute-start | bytes 393224 | tf_op jit(solution)/shard_map/ppermute | solution.py:251
  29.3 8.2 %collective-permute-start.13 = (bf16[2,8,64,128]{3,2,1,0:T(8,128)(2,1)S(1)}, bf16[2,8,64,128]{3,2,1,0:T(8,128)(2,1)S(1)}, u32[]{:S(2)}, u32[]{:S(2)}) collective-permute-start(bf16[2,8,64,128]{3,2,1,0:T(8,128)(2,1)S(1)} %shard_map.75.refs_0_), channel_id=1, source_target_pairs={{0,4},{1,3},{2,6},{3,1},{4,0},{5,7},{6,2},{7,5},{8,12},{9,11},{10,... | collective-permute-start | bytes 786440 | tf_op jit(solution)/shard_map/ppermute | solution.py:248
  30.9 7.7 %collective-permute-start.14 = (bf16[2,8,64,128]{3,2,1,0:T(8,128)(2,1)S(1)}, bf16[2,8,64,128]{3,2,1,0:T(8,128)(2,1)S(1)}, u32[]{:S(2)}, u32[]{:S(2)}) collective-permute-start(bf16[2,8,64,128]{3,2,1,0:T(8,128)(2,1)S(1)} %collective-permute-done.12.refs_1_), channel_id=1, source_target_pairs={{0,4},{1,3},{2,6},{3,1},{4,0},{5,7},{6,2},{7,5},{8,12},{9,11},{10,... | collective-permute-start | bytes 786440 | tf_op jit(solution)/shard_map/ppermute | solution.py:248
  33.7 7.6 %collective-permute-start.4 = (bf16[2,8,64,128]{3,2,1,0:T(8,128)(2,1)S(1)}, bf16[2,8,64,128]{3,2,1,0:T(8,128)(2,1)S(1)}, u32[]{:S(2)}, u32[]{:S(2)}) collective-permute-start(bf16[2,8,64,128]{3,2,1,0:T(8,128)(2,1)S(1)} %collective-permute-done.2.refs_0_), channel_id=1, source_target_pairs={{0,4},{1,3},{2,6},{3,1},{4,0},{5,7},{6,2},{7,5},{8,12},{9,11},{10,... | collective-permute-start | bytes 786440 | tf_op jit(solution)/shard_map/ppermute | solution.py:248
  35.2 8.9 %collective-permute-start.5 = (bf16[2,8,64,128]{3,2,1,0:T(8,128)(2,1)S(1)}, bf16[2,8,64,128]{3,2,1,0:T(8,128)(2,1)S(1)}, u32[]{:S(2)}, u32[]{:S(2)}) collective-permute-start(bf16[2,8,64,128]{3,2,1,0:T(8,128)(2,1)S(1)} %collective-permute-done.3.refs_1_), channel_id=1, source_target_pairs={{0,4},{1,3},{2,6},{3,1},{4,0},{5,7},{6,2},{7,5},{8,12},{9,11},{10,... | collective-permute-start | bytes 786440 | tf_op jit(solution)/shard_map/ppermute | solution.py:248
  35.7 1.3 %collective-permute-start.11 = (bf16[8,1,32,256]{3,2,1,0:T(8,128)(2,1)S(1)}, bf16[8,1,32,256]{3,2,1,0:T(8,128)(2,1)S(1)}, u32[]{:S(2)}, u32[]{:S(2)}) collective-permute-start(bf16[8,1,32,256]{3,2,1,0:T(8,128)(2,1)S(1)} %collective-permute-done.9.own_b), channel_id=1, source_target_pairs={{0,1},{1,0},{2,3},{3,2},{4,5},{5,4},{6,7},{7,6},{8,9},{9,8},{10,11... | collective-permute-start | bytes 393224 | tf_op jit(solution)/shard_map/ppermute | solution.py:251
  38.5 5.6 %copy-start.3 = (bf16[128,128]{1,0:T(8,128)(2,1)S(1)}, bf16[128,128]{1,0:T(8,128)(2,1)}, u32[]{:S(2)}) copy-start(bf16[128,128]{1,0:T(8,128)(2,1)} %refs_11_.1) | copy-start | bytes 98308
  46.2 1.3 %collective-permute-start.15 = (bf16[8,32,128]{2,1,0:T(8,128)(2,1)S(1)}, bf16[8,32,128]{2,1,0:T(8,128)(2,1)S(1)}, u32[]{:S(2)}, u32[]{:S(2)}) collective-permute-start(bf16[8,32,128]{2,1,0:T(8,128)(2,1)S(1)} %get-tuple-element.36), channel_id=1, source_target_pairs={{0,1},{1,0},{2,3},{3,2},{4,5},{5,4},{6,7},{7,6},{8,9},{9,8},{10,11... | collective-permute-start | bytes 196616 | tf_op jit(solution)/shard_map/ppermute | solution.py:251

commit v3 on v2

--- a/solution.py
+++ b/solution.py
@@ -13,11 +13,13 @@
 F32 = jnp.float32
 BF16 = jnp.bfloat16
 MIB = 1 << 20
+FIRST, SECOND = 0, 1
 LOG2_E = math.log2(math.e)
 
 
 def vmem_call(kernel, outs, *args, plain=(), in_hbm=False, scratch=(), scalars=(), room=4 * MIB):
-    args = [*plain, *(pltpu.with_memory_space_constraint(a, pltpu.VMEM) for a in args)]
+    args = [pltpu.with_memory_space_constraint(a, pltpu.VMEM) for a in args]
+    plain = [pltpu.with_memory_space_constraint(a, pltpu.HBM) for a in plain]
     if in_hbm:
         out_shape = [jax.ShapeDtypeStruct(*o) for o in outs]
     else:
@@ -25,19 +27,24 @@
     call = pl.pallas_call(
         kernel,
         in_specs=[pl.BlockSpec(memory_space=pltpu.SMEM)] * len(scalars)
+        + [pl.BlockSpec(memory_space=pl.ANY)] * len(plain)
         + [pl.BlockSpec(memory_space=pltpu.VMEM)] * len(args),
         out_specs=[pl.BlockSpec(memory_space=pltpu.VMEM)] * len(outs),
         out_shape=out_shape,
         scratch_shapes=scratch,
         compiler_params=pltpu.CompilerParams(vmem_limit_bytes=room),
     )
-    results = call(*scalars, *args)
+    results = call(*scalars, *plain, *args)
     return results if len(outs) > 1 else results[0]
 
 
 def my_place():
     index = lax.axis_index("col")
     return index >> 1, index & 1
+
+
+def by_core(core, on_first, on_second):
+    return on_first + core * (on_second - on_first)
 
 
 def contract_last(a, b):
@@ -52,11 +59,21 @@
     return (centred * lax.rsqrt(variance + 1e-05)).astype(BF16)
 
 
-def early_kernel(stages, pair_ref, bias_ref, own_ref, keep_ref, send_ref, packed_ref):
+def early_kernel(
+    dims, stages, pair_hbm, bias_hbm, own_ref, keep_ref, send_ref, packed_ref, pair_ref, bias_ref, sems
+):
     half_rows = own_ref.shape[0]
     _, core = my_place()
-    own_ref[...] = normalized(pair_ref[pl.ds(core * half_rows, half_rows)])
-    pack_bias(stages, bias_ref, keep_ref, send_ref, packed_ref)
+    pair_copy = pltpu.make_async_copy(
+        pair_hbm.at[pl.ds(core * half_rows, half_rows)], pair_ref, sems.at[0]
+    )
+    bias_copy = pltpu.make_async_copy(bias_hbm, bias_ref, sems.at[1])
+    pair_copy.start()
+    bias_copy.start()
+    pair_copy.wait()
+    own_ref[...] = normalized(pair_ref[...])
+    bias_copy.wait()
+    pack_bias(dims, stages, bias_ref, keep_ref, send_ref, packed_ref)
 
 
 def norm_kernel(own_ref, other_ref, block_ref):
@@ -93,18 +110,16 @@
     gate_ref[...] = gate.reshape(rows, cols, chans)
 
 
-def pack_bias(stages, bias_ref, keep_ref, send_ref, packed_ref):
+def pack_bias(dims, stages, bias_ref, keep_ref, send_ref, packed_ref):
     half = keep_ref.shape[1]
     chips, _, lanes = packed_ref.shape
     cols = lanes // HEADS
     chip, core = my_place()
+    shifts = [by_core(core, *(bit.bit_length() - 1 for bit in dims[stage])) for stage in stages]
     for target in range(chips):
         apart = chip ^ target
         spot = 0
-        for stage in stages:
-            shift = {"first": core, "second": 1 - core}.get(stage)
-            if shift is None:
-                shift = stage.bit_length() - 1
+        for shift in shifts:
             spot = spot * 2 + ((apart >> shift) & 1)
         for head in range(HEADS):
             packed_ref[spot, :, head * cols : (head + 1) * cols] = bias_ref[
@@ -123,23 +138,25 @@
     next_send_ref[sources:] = recv_ref[:, half:]
 
 
-def bias_kernel(offsets, spots, limit_ref, own_a, own_b, other_a, other_b, bias_ref, keys_ref):
+def bias_kernel(dims, offsets, held_at, limit_ref, own_a, own_b, other_a, other_b, bias_ref, keys_ref):
     sources, _, width, lanes = own_a.shape
     chip, core = my_place()
     limit = limit_ref[0]
-    steps = (0, 1 + core, 2 - core, 3)
-    flipped = (0, 2, 1, 3)
+    apart = [by_core(core, *pair) for pair in dims]
     row_at = lax.broadcasted_iota(jnp.int32, (width, lanes), 0)
-    for spot, (far, near) in enumerate(offsets):
-        source = chip ^ far ^ steps[near]
+    for spot, taken in enumerate(offsets):
+        source = chip
+        for dim in taken:
+            source = source ^ apart[dim]
+        mirrored = frozenset(dims.index(dims[dim][::-1]) for dim in taken)
         for parts, part, seen in (
-            ((own_a, own_b), core, near),
-            ((other_a, other_b), 1 - core, flipped[near]),
+            ((own_a, own_b), core, taken),
+            ((other_a, other_b), 1 - core, mirrored),
         ):
             first_key = (source * 2 + part) * width
             mask = jnp.where(first_key + row_at < limit, 0.0, -1000000000.0).astype(F32)
             at = pl.multiple_of(spot * 2 * width + part * width, width)
-            held = spots[far, seen]
+            held = held_at[seen]
             value = parts[held // sources][held % sources, 0]
             keys_ref[pl.ds(at, width), :] = (value.astype(F32) + mask) * LOG2_E
     bias_ref[...] = keys_ref[...].T
@@ -178,8 +195,8 @@
 
 
 def near_kernel(*refs):
-    pieces = refs[:4]
-    query_ref, bias_ref, top_ref, total_ref, mixed_ref = refs[4:]
+    pieces = refs[:-5]
+    query_ref, bias_ref, top_ref, total_ref, mixed_ref = refs[-5:]
 
     def finish(row, top, total, mixed):
         top_ref[row] = jnp.broadcast_to(top, mixed.shape)
@@ -240,48 +257,64 @@
     lanes = HEADS * cols
     chips = n_dev // 2
 
-    def swap(value, stage):
-        def partner(d):
-            apart = {"first": 1 + d % 2, "second": 2 - d % 2}.get(stage, stage)
-            return ((d // 2) ^ apart) * 2 + d % 2
-
-        return lax.ppermute(value, "col", [(d, partner(d)) for d in range(n_dev)])
+    def swap(value, dim):
+        perm = [(d, ((d // 2) ^ dims[dim][d % 2]) * 2 + d % 2) for d in range(n_dev)]
+        return lax.ppermute(value, "col", perm)
 
     def swap_core(value):
         return lax.ppermute(value, "col", [(d, d ^ 1) for d in range(n_dev)])
 
-    def spread(piece):
-        first = swap(piece, "first")
-        second = swap(piece, "second")
-        third = swap(first, "second")
-        return [piece, first, second, third]
-
-    far_bits, stages = travel(n_dev)
+    def stack(first, second):
+        shape = (first.shape[0] + second.shape[0],) + first.shape[1:]
+        return vmem_call(stack_kernel, [(shape, BF16)], first, second)
+
+    def spread(piece, offsets):
+        first = swap(piece, FIRST)
+        second = swap(stack(piece, first), SECOND)
+        return [piece, first, second], plane(offsets)
+
+    def spread_apart(piece, offsets):
+        first = swap(piece, FIRST)
+        second = swap(piece, SECOND)
+        third = swap(first, SECOND)
+        return [piece, first, second, third], plane(offsets)
+
+    def plane(offsets):
+        steps = ((), (FIRST,), (SECOND,), (FIRST, SECOND))
+        return [taken.union(step) for step in steps for taken in offsets]
+
+    dims, stages = travel(n_dev)
+    far_dims = range(2, len(dims))
 
     other = swap_core(pair)
     half_targets = ((1, chips // 2, width, lanes), BF16)
     own, keep_bias, send_bias = vmem_call(
-        functools.partial(early_kernel, stages),
+        functools.partial(early_kernel, dims, stages),
         [((half_rows, width, chans), BF16), half_targets, half_targets],
         plain=[pair, pair_bias],
-        scratch=[pltpu.VMEM((chips, width, lanes), BF16)],
-        room=4 * MIB + 4 * chips * width * lanes,
+        scratch=[
+            pltpu.VMEM((chips, width, lanes), BF16),
+            pltpu.VMEM((half_rows, width, chans), BF16),
+            pltpu.VMEM(pair_bias.shape, BF16),
+            pltpu.SemaphoreType.DMA((2,)),
+        ],
+        room=4 * MIB + 8 * chips * width * lanes,
     )
     near = vmem_call(norm_kernel, [((1, half_rows, cols, chans), BF16)], own, other)
     block = near
 
-    near_offsets = [0]
-    for bit in far_bits[:0:-1]:
-        arrived = swap(near, bit)
-        shape = (2 * near.shape[0],) + near.shape[1:]
-        near = vmem_call(stack_kernel, [(shape, BF16)], near, arrived)
-        near_offsets = near_offsets + [f ^ bit for f in near_offsets]
-    far = swap(near, far_bits[0])
-    far_offsets = [f ^ far_bits[0] for f in near_offsets]
-
-    near_pieces = spread(near)
-    far_pieces = spread(far)
-    offsets = [(f, s) for group in (near_offsets, far_offsets) for s in range(4) for f in group]
+    near_offsets = [frozenset()]
+    near_pieces, offsets = spread(block, near_offsets)
+    for dim in far_dims[:-1]:
+        arrived = swap(near, dim)
+        near = stack(near, arrived)
+        arrived_offsets = [taken | {dim} for taken in near_offsets]
+        pieces, order = spread(arrived, arrived_offsets)
+        near_pieces, offsets = near_pieces + pieces, offsets + order
+        near_offsets = near_offsets + arrived_offsets
+    far = swap(near, far_dims[-1])
+    far_pieces, order = spread_apart(far, [taken | {far_dims[-1]} for taken in near_offsets])
+    offsets = offsets + order
 
     for stage in stages[:-1]:
         recv_bias = swap(send_bias, stage)
@@ -289,11 +322,10 @@
         shape = (2 * sources, targets // 2, width, lanes)
         keep_bias, send_bias = vmem_call(trade_kernel, [(shape, BF16)] * 2, keep_bias, recv_bias)
     recv_bias = swap(send_bias, stages[-1])
-    spots = {}
-    for held in range(chips):
-        taken = [stage for k, stage in enumerate(stages) if held >> k & 1]
-        near_step = ("first" in taken) + 2 * ("second" in taken)
-        spots[sum(t for t in taken if not isinstance(t, str)), near_step] = held
+    held_at = {
+        frozenset(dim for k, dim in enumerate(stages) if held >> k & 1): held
+        for held in range(chips)
+    }
 
     query, gate = vmem_call(
         query_kernel,
@@ -302,7 +334,7 @@
     )
     n_keys = chips * cols
     bias = vmem_call(
-        functools.partial(bias_kernel, offsets, spots),
+        functools.partial(bias_kernel, dims, offsets, held_at),
         [((lanes, n_keys), F32)],
         keep_bias, recv_bias,
         swap_core(keep_bias), swap_core(recv_bias),
@@ -332,7 +364,8 @@
 def travel(n_dev):
     chips = n_dev // 2
     far_bits = [4 << k for k in range((chips // 4).bit_length() - 1)]
-    return far_bits, far_bits[:-1] + ["first", "second"] + far_bits[-1:]
+    dims = [(1, 2), (2, 1)] + list(zip(far_bits[::-1], far_bits))
+    return dims, list(range(len(dims)))
 
 
 def solution(mesh):

time: 48.4 us -> 46.9 us (0.969)
  waiting for transfers between devices: 20.5 us -> 17 us
  starting transfers between devices: 19.1 us -> 22 us
  local copies, waits for them, and re-layouts: 1.87 us -> 0.02 us
  Pallas kernels: 5.87 us -> 6.84 us
    ppermute x12 -> x13, waiting for transfers between devices: 19.1 us -> 15.6 us  [swap(): return lax.ppermute(value, 'col', perm)]
    ppermute x12 -> x13, starting transfers between devices: 18.6 us -> 21.3 us  [swap(): return lax.ppermute(value, 'col', perm)]
    unnamed x12 -> x8, local copies, waits for them, and re-layouts: 1.87 us -> 0.02 us
    pallas_call x11 -> x13, Pallas kernels: 5.87 us -> 6.84 us  [vmem_call(): results = call(*scalars, *plain, *args)]
  transfers between devices with their start and end apart: 16 -> 17, of which waited for: 9 -> 10; matrix products, arithmetic and copies ran while one was open for 0% -> 0% of each run, Pallas kernels for 6% -> 8%
where the time goes in v3:
time: 46.9 us; the launch traced here: 46.7 us
  starting transfers between devices  22 us (47%)
  waiting for transfers between devices  17 us (36%)
  Pallas kernels  6.84 us (15%)
  between operations  0.83 us (2%)
    ppermute x13, starting transfers between devices, swap(): return lax.ppermute(value, 'col', perm)  21.3 us
    ppermute x13, waiting for transfers between devices, swap(): return lax.ppermute(value, 'col', perm)  15.6 us
    pallas_call x13, Pallas kernels, vmem_call(): results = call(*scalars, *plain, *args)  6.84 us
    ppermute x4, waiting for transfers between devices, swap_core(): return lax.ppermute(value, 'col', [(d, d ^ 1) for d in range(n_dev)])  1.42 us
  transfers between devices with their start and end apart: 17, of which 10 were waited for; matrix products, arithmetic and copies ran while one was open for 0% of the time, Pallas kernels for 8%

profile of v3, /device:TPU:0, one launch (start us, length us, event | category | flops | bytes accessed | tf_op | source)
XLA Modules:
  0.0 46.7 jit_solution(12329383982313950231)
XLA Ops:
  0.0 0.5 %collective-permute-start = (bf16[16,32,128]{2,1,0:T(8,128)(2,1)}, bf16[16,32,128]{2,1,0:T(8,128)(2,1)S(1)}, u32[]{:S(2)}, u32[]{:S(2)}) collective-permute-start(bf16[16,32,128]{2,1,0:T(8,128)(2,1)} %pair_hbm.1), channel_id=1, source_target_pairs={{0,1},{1,0},{2,3},{3,2},{4,5},{5,4},{6,7},{7,6},{8,9},{9,8},{10,11... | collective-permute-start | bytes 393224 | tf_op jit(solution)/shard_map/ppermute | solution.py:265
  0.5 1.3 %shard_map.73 = (bf16[8,32,128]{2,1,0:T(8,128)(2,1)S(1)}, bf16[1,8,32,256]{3,2,1,0:T(8,128)(2,1)S(1)}, bf16[1,8,32,256]{3,2,1,0:T(8,128)(2,1)S(1)}) custom-call(bf16[16,32,128]{2,1,0:T(8,128)(2,1)} %pair_hbm.1, bf16[4,32,1024]{2,1,0:T(8,128)(2,1)} %bias_hbm.1), custom_call_target="tpu_custom_call" | custom-call | tf_op jit(solution)/shard_map/pallas_call | solution.py:37
  1.8 0.0 collective-permute-done.other_ref
  1.8 0.2 shard_map.74.first_ref.block_ref.refs_0_
  2.0 3.9 %collective-permute-start.1 = (bf16[1,8,64,128]{3,2,1,0:T(8,128)(2,1)S(1)}, bf16[1,8,64,128]{3,2,1,0:T(8,128)(2,1)S(1)}, u32[]{:S(2)}, u32[]{:S(2)}) collective-permute-start(bf16[1,8,64,128]{3,2,1,0:T(8,128)(2,1)S(1)} %shard_map.74.first_ref.block_ref.refs_0_), channel_id=1, source_target_pairs={{0,16},{1,9},{2,18},{3,11},{4,20},{5,13},{6,22},{7,15},{8,24},{9,1... | collective-permute-start | bytes 393224 | tf_op jit(solution)/shard_map/ppermute | solution.py:262
  5.9 1.5 %collective-permute-start.6 = (bf16[1,8,32,256]{3,2,1,0:T(8,128)(2,1)S(1)}, bf16[1,8,32,256]{3,2,1,0:T(8,128)(2,1)S(1)}, u32[]{:S(2)}, u32[]{:S(2)}) collective-permute-start(bf16[1,8,32,256]{3,2,1,0:T(8,128)(2,1)S(1)} %get-tuple-element.24), channel_id=1, source_target_pairs={{0,2},{1,5},{2,0},{3,7},{4,6},{5,1},{6,4},{7,3},{8,10},{9,13},{10,... | collective-permute-start | bytes 393224 | tf_op jit(solution)/shard_map/ppermute | solution.py:262
  7.4 1.5 %collective-permute-done.1.second_ref.first_ref.refs_3_ = bf16[1,8,64,128]{3,2,1,0:T(8,128)(2,1)S(1)} collective-permute-done((bf16[1,8,64,128]{3,2,1,0:T(8,128)(2,1)S(1)}, bf16[1,8,64,128]{3,2,1,0:T(8,128)(2,1)S(1)}, u32[]{:S(2)}, u32[]{:S(2)}) %collective-permute-start.1) | collective-permute-done | bytes 131104 | tf_op jit(solution)/shard_map/ppermute | solution.py:262
  8.9 2.7 %collective-permute-start.2 = (bf16[2,8,64,128]{3,2,1,0:T(8,128)(2,1)S(1)}, bf16[2,8,64,128]{3,2,1,0:T(8,128)(2,1)S(1)}, u32[]{:S(2)}, u32[]{:S(2)}) collective-permute-start(bf16[2,8,64,128]{3,2,1,0:T(8,128)(2,1)S(1)} %shard_map.75), channel_id=1, source_target_pairs={{0,8},{1,17},{2,10},{3,19},{4,12},{5,21},{6,14},{7,23},{8,0},{9,25... | collective-permute-start | bytes 786440 | tf_op jit(solution)/shard_map/ppermute | solution.py:262
  11.6 0.0 collective-permute-done.6.recv_ref
  11.7 1.6 %collective-permute-start.7 = (bf16[2,4,32,256]{3,2,1,0:T(8,128)(2,1)S(1)}, bf16[2,4,32,256]{3,2,1,0:T(8,128)(2,1)S(1)}, u32[]{:S(2)}, u32[]{:S(2)}) collective-permute-start(bf16[2,4,32,256]{3,2,1,0:T(8,128)(2,1)S(1)} %get-tuple-element.26), channel_id=1, source_target_pairs={{0,4},{1,3},{2,6},{3,1},{4,0},{5,7},{6,2},{7,5},{8,12},{9,11},{10,... | collective-permute-start | bytes 393224 | tf_op jit(solution)/shard_map/ppermute | solution.py:262
  13.2 3.4 %collective-permute-done.7.recv_ref = bf16[2,4,32,256]{3,2,1,0:T(8,128)(2,1)S(1)} collective-permute-done((bf16[2,4,32,256]{3,2,1,0:T(8,128)(2,1)S(1)}, bf16[2,4,32,256]{3,2,1,0:T(8,128)(2,1)S(1)}, u32[]{:S(2)}, u32[]{:S(2)}) %collective-permute-start.7) | collective-permute-done | bytes 131104 | tf_op jit(solution)/shard_map/ppermute | solution.py:262
  16.7 3.1 %collective-permute-start.8 = (bf16[4,2,32,256]{3,2,1,0:T(8,128)(2,1)S(1)}, bf16[4,2,32,256]{3,2,1,0:T(8,128)(2,1)S(1)}, u32[]{:S(2)}, u32[]{:S(2)}) collective-permute-start(bf16[4,2,32,256]{3,2,1,0:T(8,128)(2,1)S(1)} %get-tuple-element.28), channel_id=1, source_target_pairs={{0,16},{1,9},{2,18},{3,11},{4,20},{5,13},{6,22},{7,15},{8,24},{9,1... | collective-permute-start | bytes 393224 | tf_op jit(solution)/shard_map/ppermute | solution.py:262
  19.9 0.0 collective-permute-done.2.refs_0_
  19.9 1.5 %collective-permute-start.3 = (bf16[2,8,64,128]{3,2,1,0:T(8,128)(2,1)S(1)}, bf16[2,8,64,128]{3,2,1,0:T(8,128)(2,1)S(1)}, u32[]{:S(2)}, u32[]{:S(2)}) collective-permute-start(bf16[2,8,64,128]{3,2,1,0:T(8,128)(2,1)S(1)} %collective-permute-done.2.refs_0_), channel_id=1, source_target_pairs={{0,2},{1,5},{2,0},{3,7},{4,6},{5,1},{6,4},{7,3},{8,10},{9,13},{10,... | collective-permute-start | bytes 786440 | tf_op jit(solution)/shard_map/ppermute | solution.py:262
  21.4 0.5 %collective-permute-start.12 = (bf16[1,8,64,128]{3,2,1,0:T(8,128)(2,1)S(1)}, bf16[1,8,64,128]{3,2,1,0:T(8,128)(2,1)S(1)}, u32[]{:S(2)}, u32[]{:S(2)}) collective-permute-start(bf16[1,8,64,128]{3,2,1,0:T(8,128)(2,1)S(1)} %shard_map.74.first_ref.block_ref.refs_0_), channel_id=1, source_target_pairs={{0,2},{1,5},{2,0},{3,7},{4,6},{5,1},{6,4},{7,3},{8,10},{9,13},{10,... | collective-permute-start | bytes 393224 | tf_op jit(solution)/shard_map/ppermute | solution.py:262
  21.9 1.5 %collective-permute-start.14 = (bf16[1,8,64,128]{3,2,1,0:T(8,128)(2,1)S(1)}, bf16[1,8,64,128]{3,2,1,0:T(8,128)(2,1)S(1)}, u32[]{:S(2)}, u32[]{:S(2)}) collective-permute-start(bf16[1,8,64,128]{3,2,1,0:T(8,128)(2,1)S(1)} %collective-permute-done.1.second_ref.first_ref.refs_3_), channel_id=1, source_target_pairs={{0,2},{1,5},{2,0},{3,7},{4,6},{5,1},{6,4},{7,3},{8,10},{9,13},{10,... | collective-permute-start | bytes 393224 | tf_op jit(solution)/shard_map/ppermute | solution.py:262
  23.4 2.6 %collective-permute-done.8.recv_ref = bf16[4,2,32,256]{3,2,1,0:T(8,128)(2,1)S(1)} collective-permute-done((bf16[4,2,32,256]{3,2,1,0:T(8,128)(2,1)S(1)}, bf16[4,2,32,256]{3,2,1,0:T(8,128)(2,1)S(1)}, u32[]{:S(2)}, u32[]{:S(2)}) %collective-permute-start.8) | collective-permute-done | bytes 131104 | tf_op jit(solution)/shard_map/ppermute | solution.py:262
  26.0 0.1 collective-permute-start.9
  26.1 1.5 %collective-permute-done.12.second_ref.refs_1_ = bf16[1,8,64,128]{3,2,1,0:T(8,128)(2,1)S(1)} collective-permute-done((bf16[1,8,64,128]{3,2,1,0:T(8,128)(2,1)S(1)}, bf16[1,8,64,128]{3,2,1,0:T(8,128)(2,1)S(1)}, u32[]{:S(2)}, u32[]{:S(2)}) %collective-permute-start.12) | collective-permute-done | bytes 131104 | tf_op jit(solution)/shard_map/ppermute | solution.py:262
  27.7 0.0 copy-start
  27.7 0.0 copy-start.2
  27.7 0.0 copy-start.3
  27.7 0.1 collective-permute-start.10
  27.8 1.6 %collective-permute-start.13 = (bf16[2,8,64,128]{3,2,1,0:T(8,128)(2,1)S(1)}, bf16[2,8,64,128]{3,2,1,0:T(8,128)(2,1)S(1)}, u32[]{:S(2)}, u32[]{:S(2)}) collective-permute-start(bf16[2,8,64,128]{3,2,1,0:T(8,128)(2,1)S(1)} %shard_map.81), channel_id=1, source_target_pairs={{0,4},{1,3},{2,6},{3,1},{4,0},{5,7},{6,2},{7,5},{8,12},{9,11},{10,... | collective-permute-start | bytes 786440 | tf_op jit(solution)/shard_map/ppermute | solution.py:262
  29.4 0.0 collective-permute-done.14.second_ref.refs_4_
  29.4 1.3 %collective-permute-start.15 = (bf16[2,8,64,128]{3,2,1,0:T(8,128)(2,1)S(1)}, bf16[2,8,64,128]{3,2,1,0:T(8,128)(2,1)S(1)}, u32[]{:S(2)}, u32[]{:S(2)}) collective-permute-start(bf16[2,8,64,128]{3,2,1,0:T(8,128)(2,1)S(1)} %shard_map.82), channel_id=1, source_target_pairs={{0,4},{1,3},{2,6},{3,1},{4,0},{5,7},{6,2},{7,5},{8,12},{9,11},{10,... | collective-permute-start | bytes 786440 | tf_op jit(solution)/shard_map/ppermute | solution.py:262
  30.7 0.4 collective-permute-done.9.own_b
  31.1 2.0 %collective-permute-start.4 = (bf16[2,8,64,128]{3,2,1,0:T(8,128)(2,1)S(1)}, bf16[2,8,64,128]{3,2,1,0:T(8,128)(2,1)S(1)}, u32[]{:S(2)}, u32[]{:S(2)}) collective-permute-start(bf16[2,8,64,128]{3,2,1,0:T(8,128)(2,1)S(1)} %collective-permute-done.2.refs_0_), channel_id=1, source_target_pairs={{0,4},{1,3},{2,6},{3,1},{4,0},{5,7},{6,2},{7,5},{8,12},{9,11},{10,... | collective-permute-start | bytes 786440 | tf_op jit(solution)/shard_map/ppermute | solution.py:262
  33.1 0.0 collective-permute-done.3.refs_1_
  33.1 0.0 collective-permute-start.5
  33.1 0.0 collective-permute-done.10.other_a
  33.1 0.1 collective-permute-start.11
  33.8 0.0 copy-done
  33.8 0.0 copy-done.2
  33.8 0.0 copy-done.3
  33.8 0.5 %shard_map.76 = (bf16[8,256,128]{2,1,0:T(8,128)(2,1)S(1)}, f32[8,64,128]{2,1,0:T(8,128)S(1)}) custom-call(bf16[1,8,64,128]{3,2,1,0:T(8,128)(2,1)S(1)} %shard_map.74.first_ref.block_ref.refs_0_, bf16[128,128]{1,0:T(8,128)(2,1)S(1)} %copy-done.2, bf16[128,256]{1,0:T(8,128)(2,1)S(1)} %copy-done, bf16[128,128]{1,0:T(8,128)(2,1)S(1)} %copy-done.3), custom_call_target="tpu_custom_call" | custom-call | tf_op jit(solution)/shard_map/pallas_call | solution.py:37
  34.3 0.2 collective-permute-done.11.other_b
  34.5 0.5 %shard_map.80.refs_7_.refs_5_ = f32[256,1024]{1,0:T(8,128)S(1)} custom-call(s32[1]{0:T(128)S(6)} %copy.8.limit_ref, bf16[8,1,32,256]{3,2,1,0:T(8,128)(2,1)S(1)} %get-tuple-element.29.own_a, bf16[8,1,32,256]{3,2,1,0:T(8,128)(2,1)S(1)} %collective-permute-done.9.own_b, bf16[8,1,32,256]{3,2,1,0:T(8,128)(2,1)S(1)} %collective-permute-done.10.other_a, ...), custom_call_target="tpu_custom_call" | custom-call | tf_op jit(solution)/shard_map/pallas_call | solution.py:37
  35.0 0.0 collective-permute-done.13.refs_2_
  35.0 2.0 %collective-permute-done.15.refs_5_ = bf16[2,8,64,128]{3,2,1,0:T(8,128)(2,1)S(1)} collective-permute-done((bf16[2,8,64,128]{3,2,1,0:T(8,128)(2,1)S(1)}, bf16[2,8,64,128]{3,2,1,0:T(8,128)(2,1)S(1)}, u32[]{:S(2)}, u32[]{:S(2)}) %collective-permute-start.15) | collective-permute-done | bytes 262176 | tf_op jit(solution)/shard_map/ppermute | solution.py:262
  37.0 0.0 copy-start.1
  37.0 1.6 %shard_map.83 = (f32[8,256,128]{2,1,0:T(8,128)S(1)}, f32[8,256,128]{2,1,0:T(8,128)S(1)}, f32[8,256,128]{2,1,0:T(8,128)S(1)}) custom-call(bf16[1,8,64,128]{3,2,1,0:T(8,128)(2,1)S(1)} %shard_map.74.first_ref.block_ref.refs_0_, bf16[1,8,64,128]{3,2,1,0:T(8,128)(2,1)S(1)} %collective-permute-done.12.second_ref.refs_1_, ...), custom_call_target="tpu_custom_call" | custom-call | tf_op jit(solution)/shard_map/pallas_call | solution.py:37
  38.6 1.2 %collective-permute-done.4.refs_2_ = bf16[2,8,64,128]{3,2,1,0:T(8,128)(2,1)S(1)} collective-permute-done((bf16[2,8,64,128]{3,2,1,0:T(8,128)(2,1)S(1)}, bf16[2,8,64,128]{3,2,1,0:T(8,128)(2,1)S(1)}, u32[]{:S(2)}, u32[]{:S(2)}) %collective-permute-start.4) | collective-permute-done | bytes 262176 | tf_op jit(solution)/shard_map/ppermute | solution.py:262
  39.8 2.8 %collective-permute-done.5.refs_3_ = bf16[2,8,64,128]{3,2,1,0:T(8,128)(2,1)S(1)} collective-permute-done((bf16[2,8,64,128]{3,2,1,0:T(8,128)(2,1)S(1)}, bf16[2,8,64,128]{3,2,1,0:T(8,128)(2,1)S(1)}, u32[]{:S(2)}, u32[]{:S(2)}) %collective-permute-start.5) | collective-permute-done | bytes 262176 | tf_op jit(solution)/shard_map/ppermute | solution.py:262
  42.6 0.0 copy-done.1
  42.6 2.1 %shard_map.84 = (bf16[8,32,128]{2,1,0:T(8,128)(2,1)S(1)}, bf16[8,32,128]{2,1,0:T(8,128)(2,1)S(1)}) custom-call(bf16[2,8,64,128]{3,2,1,0:T(8,128)(2,1)S(1)} %collective-permute-done.2.refs_0_, bf16[2,8,64,128]{3,2,1,0:T(8,128)(2,1)S(1)} %collective-permute-done.3.refs_1_, bf16[2,8,64,128]{3,2,1,0:T(8,128)(2,1)S(1)} %collective-permute-done.4.refs_2_, ...), custom_call_target="tpu_custom_call" | custom-call | tf_op jit(solution)/shard_map/pallas_call | solution.py:37
  44.7 0.1 collective-permute-start.16
  44.8 1.2 %collective-permute-done.16.recv_ref = bf16[8,32,128]{2,1,0:T(8,128)(2,1)S(1)} collective-permute-done((bf16[8,32,128]{2,1,0:T(8,128)(2,1)S(1)}, bf16[8,32,128]{2,1,0:T(8,128)(2,1)S(1)}, u32[]{:S(2)}, u32[]{:S(2)}) %collective-permute-start.16) | collective-permute-done | bytes 65568 | tf_op jit(solution)/shard_map/ppermute | solution.py:265
  46.0 0.7 %shard_map.85 = bf16[16,32,128]{2,1,0:T(8,128)(2,1)} custom-call(bf16[8,32,128]{2,1,0:T(8,128)(2,1)S(1)} %get-tuple-element.35.keep_ref, bf16[8,32,128]{2,1,0:T(8,128)(2,1)S(1)} %collective-permute-done.16.recv_ref), custom_call_target="tpu_custom_call" | custom-call | tf_op jit(solution)/shard_map/pallas_call | solution.py:37
  (6 shorter events, 0.1 us)
Async XLA Ops:
  0.0 1.8 %collective-permute-start = (bf16[16,32,128]{2,1,0:T(8,128)(2,1)}, bf16[16,32,128]{2,1,0:T(8,128)(2,1)S(1)}, u32[]{:S(2)}, u32[]{:S(2)}) collective-permute-start(bf16[16,32,128]{2,1,0:T(8,128)(2,1)} %pair_hbm.1), channel_id=1, source_target_pairs={{0,1},{1,0},{2,3},{3,2},{4,5},{5,4},{6,7},{7,6},{8,9},{9,8},{10,11... | collective-permute-start | bytes 393224 | tf_op jit(solution)/shard_map/ppermute | solution.py:265
  2.0 6.9 %collective-permute-start.1 = (bf16[1,8,64,128]{3,2,1,0:T(8,128)(2,1)S(1)}, bf16[1,8,64,128]{3,2,1,0:T(8,128)(2,1)S(1)}, u32[]{:S(2)}, u32[]{:S(2)}) collective-permute-start(bf16[1,8,64,128]{3,2,1,0:T(8,128)(2,1)S(1)} %shard_map.74.first_ref.block_ref.refs_0_), channel_id=1, source_target_pairs={{0,16},{1,9},{2,18},{3,11},{4,20},{5,13},{6,22},{7,15},{8,24},{9,1... | collective-permute-start | bytes 393224 | tf_op jit(solution)/shard_map/ppermute | solution.py:262
  5.9 5.7 %collective-permute-start.6 = (bf16[1,8,32,256]{3,2,1,0:T(8,128)(2,1)S(1)}, bf16[1,8,32,256]{3,2,1,0:T(8,128)(2,1)S(1)}, u32[]{:S(2)}, u32[]{:S(2)}) collective-permute-start(bf16[1,8,32,256]{3,2,1,0:T(8,128)(2,1)S(1)} %get-tuple-element.24), channel_id=1, source_target_pairs={{0,2},{1,5},{2,0},{3,7},{4,6},{5,1},{6,4},{7,3},{8,10},{9,13},{10,... | collective-permute-start | bytes 393224 | tf_op jit(solution)/shard_map/ppermute | solution.py:262
  8.9 10.9 %collective-permute-start.2 = (bf16[2,8,64,128]{3,2,1,0:T(8,128)(2,1)S(1)}, bf16[2,8,64,128]{3,2,1,0:T(8,128)(2,1)S(1)}, u32[]{:S(2)}, u32[]{:S(2)}) collective-permute-start(bf16[2,8,64,128]{3,2,1,0:T(8,128)(2,1)S(1)} %shard_map.75), channel_id=1, source_target_pairs={{0,8},{1,17},{2,10},{3,19},{4,12},{5,21},{6,14},{7,23},{8,0},{9,25... | collective-permute-start | bytes 786440 | tf_op jit(solution)/shard_map/ppermute | solution.py:262
  11.7 5.0 %collective-permute-start.7 = (bf16[2,4,32,256]{3,2,1,0:T(8,128)(2,1)S(1)}, bf16[2,4,32,256]{3,2,1,0:T(8,128)(2,1)S(1)}, u32[]{:S(2)}, u32[]{:S(2)}) collective-permute-start(bf16[2,4,32,256]{3,2,1,0:T(8,128)(2,1)S(1)} %get-tuple-element.26), channel_id=1, source_target_pairs={{0,4},{1,3},{2,6},{3,1},{4,0},{5,7},{6,2},{7,5},{8,12},{9,11},{10,... | collective-permute-start | bytes 393224 | tf_op jit(solution)/shard_map/ppermute | solution.py:262
  16.7 9.3 %collective-permute-start.8 = (bf16[4,2,32,256]{3,2,1,0:T(8,128)(2,1)S(1)}, bf16[4,2,32,256]{3,2,1,0:T(8,128)(2,1)S(1)}, u32[]{:S(2)}, u32[]{:S(2)}) collective-permute-start(bf16[4,2,32,256]{3,2,1,0:T(8,128)(2,1)S(1)} %get-tuple-element.28), channel_id=1, source_target_pairs={{0,16},{1,9},{2,18},{3,11},{4,20},{5,13},{6,22},{7,15},{8,24},{9,1... | collective-permute-start | bytes 393224 | tf_op jit(solution)/shard_map/ppermute | solution.py:262
  19.9 13.2 %collective-permute-start.3 = (bf16[2,8,64,128]{3,2,1,0:T(8,128)(2,1)S(1)}, bf16[2,8,64,128]{3,2,1,0:T(8,128)(2,1)S(1)}, u32[]{:S(2)}, u32[]{:S(2)}) collective-permute-start(bf16[2,8,64,128]{3,2,1,0:T(8,128)(2,1)S(1)} %collective-permute-done.2.refs_0_), channel_id=1, source_target_pairs={{0,2},{1,5},{2,0},{3,7},{4,6},{5,1},{6,4},{7,3},{8,10},{9,13},{10,... | collective-permute-start | bytes 786440 | tf_op jit(solution)/shard_map/ppermute | solution.py:262
  21.4 6.3 %collective-permute-start.12 = (bf16[1,8,64,128]{3,2,1,0:T(8,128)(2,1)S(1)}, bf16[1,8,64,128]{3,2,1,0:T(8,128)(2,1)S(1)}, u32[]{:S(2)}, u32[]{:S(2)}) collective-permute-start(bf16[1,8,64,128]{3,2,1,0:T(8,128)(2,1)S(1)} %shard_map.74.first_ref.block_ref.refs_0_), channel_id=1, source_target_pairs={{0,2},{1,5},{2,0},{3,7},{4,6},{5,1},{6,4},{7,3},{8,10},{9,13},{10,... | collective-permute-start | bytes 393224 | tf_op jit(solution)/shard_map/ppermute | solution.py:262
  21.9 7.5 %collective-permute-start.14 = (bf16[1,8,64,128]{3,2,1,0:T(8,128)(2,1)S(1)}, bf16[1,8,64,128]{3,2,1,0:T(8,128)(2,1)S(1)}, u32[]{:S(2)}, u32[]{:S(2)}) collective-permute-start(bf16[1,8,64,128]{3,2,1,0:T(8,128)(2,1)S(1)} %collective-permute-done.1.second_ref.first_ref.refs_3_), channel_id=1, source_target_pairs={{0,2},{1,5},{2,0},{3,7},{4,6},{5,1},{6,4},{7,3},{8,10},{9,13},{10,... | collective-permute-start | bytes 393224 | tf_op jit(solution)/shard_map/ppermute | solution.py:262
  26.0 5.0 %collective-permute-start.9 = (bf16[8,1,32,256]{3,2,1,0:T(8,128)(2,1)S(1)}, bf16[8,1,32,256]{3,2,1,0:T(8,128)(2,1)S(1)}, u32[]{:S(2)}, u32[]{:S(2)}) collective-permute-start(bf16[8,1,32,256]{3,2,1,0:T(8,128)(2,1)S(1)} %get-tuple-element.30), channel_id=1, source_target_pairs={{0,8},{1,17},{2,10},{3,19},{4,12},{5,21},{6,14},{7,23},{8,0},{9,25... | collective-permute-start | bytes 393224 | tf_op jit(solution)/shard_map/ppermute | solution.py:262
  27.7 6.2 %copy-start = (bf16[128,256]{1,0:T(8,128)(2,1)S(1)}, bf16[128,256]{1,0:T(8,128)(2,1)}, u32[]{:S(2)}) copy-start(bf16[128,256]{1,0:T(8,128)(2,1)} %refs_10_.1) | copy-start | bytes 196612
  27.7 6.2 %copy-start.2 = (bf16[128,128]{1,0:T(8,128)(2,1)S(1)}, bf16[128,128]{1,0:T(8,128)(2,1)}, u32[]{:S(2)}) copy-start(bf16[128,128]{1,0:T(8,128)(2,1)} %w_query_ref.1) | copy-start | bytes 98308
  27.7 6.2 %copy-start.3 = (bf16[128,128]{1,0:T(8,128)(2,1)S(1)}, bf16[128,128]{1,0:T(8,128)(2,1)}, u32[]{:S(2)}) copy-start(bf16[128,128]{1,0:T(8,128)(2,1)} %w_gate_ref.1) | copy-start | bytes 98308
  27.7 5.4 %collective-permute-start.10 = (bf16[8,1,32,256]{3,2,1,0:T(8,128)(2,1)S(1)}, bf16[8,1,32,256]{3,2,1,0:T(8,128)(2,1)S(1)}, u32[]{:S(2)}, u32[]{:S(2)}) collective-permute-start(bf16[8,1,32,256]{3,2,1,0:T(8,128)(2,1)S(1)} %get-tuple-element.29.own_a), channel_id=1, source_target_pairs={{0,1},{1,0},{2,3},{3,2},{4,5},{5,4},{6,7},{7,6},{8,9},{9,8},{10,11... | collective-permute-start | bytes 393224 | tf_op jit(solution)/shard_map/ppermute | solution.py:265
  27.8 7.2 %collective-permute-start.13 = (bf16[2,8,64,128]{3,2,1,0:T(8,128)(2,1)S(1)}, bf16[2,8,64,128]{3,2,1,0:T(8,128)(2,1)S(1)}, u32[]{:S(2)}, u32[]{:S(2)}) collective-permute-start(bf16[2,8,64,128]{3,2,1,0:T(8,128)(2,1)S(1)} %shard_map.81), channel_id=1, source_target_pairs={{0,4},{1,3},{2,6},{3,1},{4,0},{5,7},{6,2},{7,5},{8,12},{9,11},{10,... | collective-permute-start | bytes 786440 | tf_op jit(solution)/shard_map/ppermute | solution.py:262
  29.4 7.6 %collective-permute-start.15 = (bf16[2,8,64,128]{3,2,1,0:T(8,128)(2,1)S(1)}, bf16[2,8,64,128]{3,2,1,0:T(8,128)(2,1)S(1)}, u32[]{:S(2)}, u32[]{:S(2)}) collective-permute-start(bf16[2,8,64,128]{3,2,1,0:T(8,128)(2,1)S(1)} %shard_map.82), channel_id=1, source_target_pairs={{0,4},{1,3},{2,6},{3,1},{4,0},{5,7},{6,2},{7,5},{8,12},{9,11},{10,... | collective-permute-start | bytes 786440 | tf_op jit(solution)/shard_map/ppermute | solution.py:262
  31.1 8.8 %collective-permute-start.4 = (bf16[2,8,64,128]{3,2,1,0:T(8,128)(2,1)S(1)}, bf16[2,8,64,128]{3,2,1,0:T(8,128)(2,1)S(1)}, u32[]{:S(2)}, u32[]{:S(2)}) collective-permute-start(bf16[2,8,64,128]{3,2,1,0:T(8,128)(2,1)S(1)} %collective-permute-done.2.refs_0_), channel_id=1, source_target_pairs={{0,4},{1,3},{2,6},{3,1},{4,0},{5,7},{6,2},{7,5},{8,12},{9,11},{10,... | collective-permute-start | bytes 786440 | tf_op jit(solution)/shard_map/ppermute | solution.py:262
  33.1 9.6 %collective-permute-start.5 = (bf16[2,8,64,128]{3,2,1,0:T(8,128)(2,1)S(1)}, bf16[2,8,64,128]{3,2,1,0:T(8,128)(2,1)S(1)}, u32[]{:S(2)}, u32[]{:S(2)}) collective-permute-start(bf16[2,8,64,128]{3,2,1,0:T(8,128)(2,1)S(1)} %collective-permute-done.3.refs_1_), channel_id=1, source_target_pairs={{0,4},{1,3},{2,6},{3,1},{4,0},{5,7},{6,2},{7,5},{8,12},{9,11},{10,... | collective-permute-start | bytes 786440 | tf_op jit(solution)/shard_map/ppermute | solution.py:262
  33.1 1.4 %collective-permute-start.11 = (bf16[8,1,32,256]{3,2,1,0:T(8,128)(2,1)S(1)}, bf16[8,1,32,256]{3,2,1,0:T(8,128)(2,1)S(1)}, u32[]{:S(2)}, u32[]{:S(2)}) collective-permute-start(bf16[8,1,32,256]{3,2,1,0:T(8,128)(2,1)S(1)} %collective-permute-done.9.own_b), channel_id=1, source_target_pairs={{0,1},{1,0},{2,3},{3,2},{4,5},{5,4},{6,7},{7,6},{8,9},{9,8},{10,11... | collective-permute-start | bytes 393224 | tf_op jit(solution)/shard_map/ppermute | solution.py:265
  37.0 5.6 %copy-start.1 = (bf16[128,128]{1,0:T(8,128)(2,1)S(1)}, bf16[128,128]{1,0:T(8,128)(2,1)}, u32[]{:S(2)}) copy-start(bf16[128,128]{1,0:T(8,128)(2,1)} %refs_11_.1) | copy-start | bytes 98308
  44.7 1.3 %collective-permute-start.16 = (bf16[8,32,128]{2,1,0:T(8,128)(2,1)S(1)}, bf16[8,32,128]{2,1,0:T(8,128)(2,1)S(1)}, u32[]{:S(2)}, u32[]{:S(2)}) collective-permute-start(bf16[8,32,128]{2,1,0:T(8,128)(2,1)S(1)} %get-tuple-element.36), channel_id=1, source_target_pairs={{0,1},{1,0},{2,3},{3,2},{4,5},{5,4},{6,7},{7,6},{8,9},{9,8},{10,11... | collective-permute-start | bytes 196616 | tf_op jit(solution)/shard_map/ppermute | solution.py:265
